TPU v7x, 1024 devices: a whole 8x8x8 slice. The times are simulated.
1024 devices in a mesh: ctx: 64 (over x, y_lo, core), head: 16 (over z, y_hi).
Axes of the slice: x: 8, y: 8 (y_hi: 2, y_lo: 4; y = y_hi * 4 + y_lo), z: 8, core: 2. Of those that a mesh axis runs over, the one named last changes fastest.
Arguments:
- query: bfloat16 [16, 8192, 2048], P('head', 'ctx'), as said below
- key: bfloat16 [16, 8192, 512], P('head', 'ctx'), as said below
- value: bfloat16 [16, 8192, 512], P('head', 'ctx'), may hold values from -6 to 6
- attn_out: bfloat16 [16, 8192, 2048], P(None, 'ctx', 'head'), may hold values from -6 to 6
- grad_out: bfloat16 [16, 8192, 2048], P('head', 'ctx'), may hold values from -24 to 24
- logsumexp: float32 [16, 8192, 16], P(None, 'ctx', 'head'), as said below
- span_order: int32 [128], replicated, may hold values from 0 to 127, as said below
Outputs:
- grad_query: bfloat16 [16, 8192, 2048], P('head', 'ctx')
- grad_key: bfloat16 [16, 8192, 512], P('head', 'ctx')
- grad_value: bfloat16 [16, 8192, 512], P('head', 'ctx')
Inputs may be any that keep to these rules, and one draw needn't show every extreme that they name: `span_order`: a permutation; the stored spans 2 d and 2 d + 1 hold sequence spans whose numbers add up to 127. logsumexp is the log of the sum over allowed keys of all cycle steps of exp of the scaled scores of query and key as given. `query`: independent entries of order one. `key`: independent entries of order one.
All inputs are finite; a program needn't handle non-finite values.
Results may differ from a plain program's by a relative error of at most 0.0095.
Values may be sent and summed in bfloat16 or wider, within the bound.
A program may use at most 32 MiB of HBM per device.

v0:
```python
import jax
import jax.numpy as jnp
from jax import lax
from jax.sharding import PartitionSpec as P

HEADS = 16
KV_HEADS = 4
HEAD_DIM = 128
CYCLE_STEPS = 3


def passed_along(value, axis, steps):
    count = lax.axis_size(axis)
    pairs = [(source, (source + steps) % count) for source in range(count)]
    return lax.ppermute(value, axis, pairs)


def shards(query, key, value, attn_out, grad_out, logsumexp, span_order):
    cycle_size = lax.axis_size("ctx")
    here = lax.axis_index("ctx")
    tok_rows = query.shape[1]
    span_rows = tok_rows // 2
    group = HEADS // KV_HEADS
    score_scale = HEAD_DIM ** (-0.5)
    offsets = jnp.arange(span_rows, dtype=jnp.int32)

    def shard_positions(shard):
        starts = lax.dynamic_slice_in_dim(span_order, 2 * shard, 2) * span_rows
        return (starts[:, None] + offsets[None, :]).reshape(tok_rows)

    key_rep = jnp.repeat(key.reshape(1, tok_rows, KV_HEADS, HEAD_DIM), group, axis=2).reshape(
        1, tok_rows, HEADS * HEAD_DIM
    )
    value_rep = jnp.repeat(value.reshape(1, tok_rows, KV_HEADS, HEAD_DIM), group, axis=2).reshape(
        1, tok_rows, HEADS * HEAD_DIM
    )
    moved = lax.all_to_all(
        jnp.stack((query, key_rep, value_rep, grad_out)),
        "head",
        split_axis=3,
        concat_axis=1,
        tiled=True,
    )
    q_rows, k_rows, v_rows, g_rows = (moved[0], moved[1], moved[2], moved[3])
    seq_count = q_rows.shape[0]
    kv_groups = q_rows.shape[2] // HEAD_DIM
    per_group = 1
    queries = q_rows.reshape(seq_count, tok_rows, kv_groups, per_group, HEAD_DIM)
    upstream = g_rows.reshape(seq_count, tok_rows, kv_groups, per_group, HEAD_DIM)
    outputs = attn_out.reshape(seq_count, tok_rows, kv_groups, per_group, HEAD_DIM)
    delta_rows = jnp.sum(outputs.astype(jnp.float32) * upstream.astype(jnp.float32), axis=4)
    delta_heads = jnp.transpose(delta_rows, (0, 2, 3, 1))
    lse_heads = jnp.transpose(
        logsumexp.reshape(seq_count, tok_rows, kv_groups, per_group), (0, 2, 3, 1)
    )
    query_pos = shard_positions(here)
    flat_shape = (seq_count, tok_rows, kv_groups * per_group * HEAD_DIM)

    def block_grads(keys_blk, values_blk, key_pos):
        keys_here = keys_blk.reshape(seq_count, tok_rows, kv_groups, HEAD_DIM)
        values_here = values_blk.reshape(seq_count, tok_rows, kv_groups, HEAD_DIM)
        scores = jnp.einsum(
            "sqgrd,skgd->sgrqk", queries, keys_here, preferred_element_type=jnp.float32
        )
        allowed = key_pos[None, :] <= query_pos[:, None]
        attn_probs = jnp.exp(
            jnp.where(allowed, scores * score_scale - lse_heads[..., None], -jnp.inf)
        )
        dprobs = jnp.einsum(
            "sqgrd,skgd->sgrqk", upstream, values_here, preferred_element_type=jnp.float32
        )
        dscores = (attn_probs * (dprobs - delta_heads[..., None])).astype(jnp.bfloat16)
        query_part = jnp.einsum(
            "sgrqk,skgd->sqgrd", dscores, keys_here, preferred_element_type=jnp.float32
        )
        key_part = (
            jnp.einsum("sgrqk,sqgrd->skgrd", dscores, queries, preferred_element_type=jnp.float32)
            * score_scale
        ).astype(jnp.bfloat16)
        value_part = jnp.einsum(
            "sgrqk,sqgrd->skgrd",
            attn_probs.astype(jnp.bfloat16),
            upstream,
            preferred_element_type=jnp.float32,
        ).astype(jnp.bfloat16)
        return (query_part, key_part.reshape(flat_shape), value_part.reshape(flat_shape))

    own_kv = jnp.stack((k_rows, v_rows))
    query_sum, key_first, value_first = block_grads(k_rows, v_rows, query_pos)
    key_sum = key_first.astype(jnp.float32)
    value_sum = value_first.astype(jnp.float32)
    kv_now = own_kv
    for step in range(1, CYCLE_STEPS):
        kv_now = passed_along(kv_now, "ctx", 1)
        source = (here - step) % cycle_size
        part_query, part_key, part_value = block_grads(
            kv_now[0], kv_now[1], shard_positions(source)
        )
        query_sum = query_sum + part_query
        returned = passed_along(jnp.stack((part_key, part_value)), "ctx", -step)
        key_sum = key_sum + returned[0].astype(jnp.float32)
        value_sum = value_sum + returned[1].astype(jnp.float32)
    query_grad = (query_sum * score_scale).astype(jnp.bfloat16).reshape(flat_shape)
    key_heads = key_sum.astype(jnp.bfloat16)
    value_heads = value_sum.astype(jnp.bfloat16)
    back = lax.all_to_all(
        jnp.stack((query_grad, key_heads, value_heads)),
        "head",
        split_axis=1,
        concat_axis=3,
        tiled=True,
    )
    q_back, k_back, v_back = (back[0], back[1], back[2])
    key_total = (
        k_back.reshape(1, tok_rows, KV_HEADS, group, HEAD_DIM)
        .astype(jnp.float32)
        .sum(axis=3)
        .reshape(1, tok_rows, KV_HEADS * HEAD_DIM)
    )
    value_total = (
        v_back.reshape(1, tok_rows, KV_HEADS, group, HEAD_DIM)
        .astype(jnp.float32)
        .sum(axis=3)
        .reshape(1, tok_rows, KV_HEADS * HEAD_DIM)
    )
    return (q_back, key_total.astype(jnp.bfloat16), value_total.astype(jnp.bfloat16))


def solution(mesh):
    in_specs = (
        P("head", "ctx", None),
        P("head", "ctx", None),
        P("head", "ctx", None),
        P(None, "ctx", "head"),
        P("head", "ctx", None),
        P(None, "ctx", "head"),
        P(),
    )
    out_specs = (P("head", "ctx", None), P("head", "ctx", None), P("head", "ctx", None))
    return jax.shard_map(shards, mesh=mesh, in_specs=in_specs, out_specs=out_specs, check_vma=False)
```

profile of v0, /device:TPU:78, one launch (start us, length us, event | category | flops | bytes accessed | tf_op | source)
XLA Modules:
  0.0 254.9 jit_solution(1808356357814936478)
XLA Ops:
  0.6 1.0 copy.128
  1.7 1.0 copy.129
  3.3 1.5 pad_maximum_fusion
  4.8 2.5 copy.85
  7.4 72.3 %all_to_all.30 = bf16[4,1,128,2048]{2,0,1,3:T(4,128)(2,1)} all-to-all(bf16[4,1,128,2048]{2,0,1,3:T(4,128)(2,1)} %copy.85), channel_id=1, replica_groups=mesh['ctx'=64,'head'=16] {'head'}, dimensions={3} | all-to-all | bytes 4194304 | tf_op jit(solution)/shard_map/all_to_all | solution.py:37
  79.7 3.2 %copy.87 = bf16[4,1,128,16,128]{4,2,3,1,0:T(8,128)(2,1)S(1)} copy(bf16[4,1,128,16,128]{2,0,4,3,1:T(4,128)(2,1)} %bitcast.267) | data formatting | bytes 4194304 | tf_op jit(solution)/shard_map/all_to_all | solution.py:37
  83.0 1.1 pad_maximum_fusion.2
  84.0 1.9 collective-permute-start
  86.6 16.4 %collective-permute-done = bf16[2,16,128,128]{3,2,1,0:T(8,128)(2,1)S(1)} collective-permute-done((bf16[2,16,128,128]{3,2,1,0:T(8,128)(2,1)}, bf16[2,16,128,128]{3,2,1,0:T(8,128)(2,1)S(1)}, u32[]{:S(2)}, u32[]{:S(2)}) %collective-permute-start) | collective-permute-done | bytes 1048608 | tf_op jit(solution)/shard_map/ppermute | solution.py:15
  103.0 1.9 collective-permute-start.1
  104.9 1.4 multiply_reduce_fusion
  106.3 0.5 fusion.20
  106.8 0.5 fusion.39
  107.3 0.5 fusion.33
  107.9 0.5 fusion.41
  108.5 6.3 %collective-permute-start.2 = (bf16[2,16,128,128]{2,3,1,0:T(8,128)(2,1)S(1)}, bf16[2,16,128,128]{2,3,1,0:T(8,128)(2,1)S(1)}, u32[]{:S(2)}, u32[]{:S(2)}) collective-permute-start(bf16[2,16,128,128]{2,3,1,0:T(8,128)(2,1)S(1)} %pad_maximum_fusion.3), channel_id=1, source_target_pairs={{0,1008},{16,0},{32,16},{48,32},{64,48},{80,64},{96,80},{112,96},{... | collective-permute-start | bytes 3145736 | tf_op jit(solution)/shard_map/ppermute | solution.py:15
  114.8 7.2 %collective-permute-done.1 = bf16[2,16,128,128]{3,2,1,0:T(8,128)(2,1)S(1)} collective-permute-done((bf16[2,16,128,128]{3,2,1,0:T(8,128)(2,1)S(1)}, bf16[2,16,128,128]{3,2,1,0:T(8,128)(2,1)S(1)}, u32[]{:S(2)}, u32[]{:S(2)}) %collective-permute-start.1) | collective-permute-done | bytes 1048608 | tf_op jit(solution)/shard_map/ppermute | solution.py:15
  122.1 0.5 fusion.24
  122.6 0.5 fusion.42
  123.1 0.5 fusion.40
  123.6 0.5 fusion.32
  124.2 1.9 collective-permute-start.3
  126.1 0.5 fusion.16
  126.6 0.5 fusion.38
  128.2 0.5 collective-permute-done.2
  128.6 27.0 %collective-permute-done.3 = bf16[2,16,128,128]{2,3,1,0:T(8,128)(2,1)S(1)} collective-permute-done((bf16[2,16,128,128]{2,3,1,0:T(8,128)(2,1)S(1)}, bf16[2,16,128,128]{2,3,1,0:T(8,128)(2,1)S(1)}, u32[]{:S(2)}, u32[]{:S(2)}) %collective-permute-start.3) | collective-permute-done | bytes 1048608 | tf_op jit(solution)/shard_map/ppermute | solution.py:15
  155.7 0.5 add_convert_fusion
  156.2 0.5 add_convert_fusion.1
  157.0 94.9 %all_to_all.31 = bf16[3,16,128,128]{2,3,0,1:T(8,128)(2,1)S(1)} all-to-all(bf16[3,16,128,128]{2,3,0,1:T(8,128)(2,1)S(1)} %copy.106), channel_id=1, replica_groups=mesh['ctx'=64,'head'=16] {'head'}, dimensions={1} | all-to-all | bytes 3145728 | tf_op jit(solution)/shard_map/all_to_all | solution.py:106
  252.2 0.8 copy.109
  253.1 0.8 copy.108
  253.8 1.0 copy.107
  (26 shorter events, 3.2 us)
Async XLA Ops:
  82.8 3.2 %copy-start = (s32[128]{0:T(128)S(1)}, s32[128]{0:T(128)}, u32[]{:S(2)}) copy-start(s32[128]{0:T(128)} %param.13) | copy-start | bytes 1540
  82.9 23.4 %copy-start.1 = (f32[16,128,1]{1,2,0:T(1,128)S(1)}, f32[16,128,1]{1,2,0:T(1,128)}, u32[]{:S(2)}) copy-start(f32[16,128,1]{1,2,0:T(1,128)} %param.12) | copy-start | bytes 24580
  84.0 19.0 %collective-permute-start = (bf16[2,16,128,128]{3,2,1,0:T(8,128)(2,1)}, bf16[2,16,128,128]{3,2,1,0:T(8,128)(2,1)S(1)}, u32[]{:S(2)}, u32[]{:S(2)}) collective-permute-start(bf16[2,16,128,128]{3,2,1,0:T(8,128)(2,1)} %pad_maximum_fusion.2), channel_id=1, source_target_pairs={{0,16},{16,32},{32,48},{48,64},{64,80},{80,96},{96,112},{112,128},... | collective-permute-start | bytes 3145736 | tf_op jit(solution)/shard_map/ppermute | solution.py:15
  103.0 19.0 %collective-permute-start.1 = (bf16[2,16,128,128]{3,2,1,0:T(8,128)(2,1)S(1)}, bf16[2,16,128,128]{3,2,1,0:T(8,128)(2,1)S(1)}, u32[]{:S(2)}, u32[]{:S(2)}) collective-permute-start(bf16[2,16,128,128]{3,2,1,0:T(8,128)(2,1)S(1)} %collective-permute-done), channel_id=1, source_target_pairs={{0,16},{16,32},{32,48},{48,64},{64,80},{80,96},{96,112},{112,128},... | collective-permute-start | bytes 3145736 | tf_op jit(solution)/shard_map/ppermute | solution.py:15
  108.5 20.2 %collective-permute-start.2 = (bf16[2,16,128,128]{2,3,1,0:T(8,128)(2,1)S(1)}, bf16[2,16,128,128]{2,3,1,0:T(8,128)(2,1)S(1)}, u32[]{:S(2)}, u32[]{:S(2)}) collective-permute-start(bf16[2,16,128,128]{2,3,1,0:T(8,128)(2,1)S(1)} %pad_maximum_fusion.3), channel_id=1, source_target_pairs={{0,1008},{16,0},{32,16},{48,32},{64,48},{80,64},{96,80},{112,96},{... | collective-permute-start | bytes 3145736 | tf_op jit(solution)/shard_map/ppermute | solution.py:15
  124.2 31.5 %collective-permute-start.3 = (bf16[2,16,128,128]{2,3,1,0:T(8,128)(2,1)S(1)}, bf16[2,16,128,128]{2,3,1,0:T(8,128)(2,1)S(1)}, u32[]{:S(2)}, u32[]{:S(2)}) collective-permute-start(bf16[2,16,128,128]{2,3,1,0:T(8,128)(2,1)S(1)} %pad_maximum_fusion.4), channel_id=1, source_target_pairs={{0,992},{16,1008},{32,0},{48,16},{64,32},{80,48},{96,64},{112,80},... | collective-permute-start | bytes 3145736 | tf_op jit(solution)/shard_map/ppermute | solution.py:15
where the time goes:
time: 255 us
  blocking collectives  167 us (65%)
  waiting for transfers between devices  51.1 us (20%)
  starting transfers between devices  12.1 us (5%)
  local copies, waits for them, and re-layouts  11.5 us (5%)
  matrix products  7.11 us (3%)
  other arithmetic  4.8 us (2%)
    all_to_all x1, blocking collectives, shards(): lax.all_to_all(jnp.stack((query_grad, key_heads, value_heads)), 'head', s...  94.9 us
    all_to_all x1, blocking collectives, shards(): lax.all_to_all(jnp.stack((query, key_rep, value_rep, grad_out)), 'head',...  72.3 us
    ppermute x4, waiting for transfers between devices, passed_along(): return lax.ppermute(value, axis, pairs)  51.1 us
    ppermute x4, starting transfers between devices, passed_along(): return lax.ppermute(value, axis, pairs)  12.1 us
  transfers between devices with their start and end apart: 4, of which 4 were waited for; matrix products, arithmetic and copies ran while one was open for 3% of the time, Pallas kernels for 0%

commit v1 on v0

v1 whole, which is shorter than its diff:
```python
import jax
import jax.numpy as jnp
from jax import lax
from jax.sharding import PartitionSpec as P

HEADS = 16
KV_HEADS = 4
HEAD_DIM = 128
CYCLE_STEPS = 3


def passed_along(value, axis, steps):
    count = lax.axis_size(axis)
    pairs = [(source, (source + steps) % count) for source in range(count)]
    return lax.ppermute(value, axis, pairs)


def shards(query, key, value, attn_out, grad_out, logsumexp, span_order):
    cycle_size = lax.axis_size("ctx")
    here = lax.axis_index("ctx")
    seq_count = query.shape[0]
    tok_rows = query.shape[1]
    span_rows = tok_rows // 2
    group = HEADS // KV_HEADS
    score_scale = HEAD_DIM ** (-0.5)
    offsets = jnp.arange(span_rows, dtype=jnp.int32)

    def shard_positions(shard):
        starts = lax.dynamic_slice_in_dim(span_order, 2 * shard, 2) * span_rows
        return (starts[:, None] + offsets[None, :]).reshape(tok_rows)

    own_kv = jnp.stack((key, value))
    kv_ahead = [passed_along(own_kv, "ctx", step) for step in range(1, CYCLE_STEPS)]

    outputs = lax.all_to_all(attn_out, "head", split_axis=0, concat_axis=2, tiled=True)
    lse_rows = lax.all_to_all(logsumexp, "head", split_axis=0, concat_axis=2, tiled=True)

    q5 = query.reshape(seq_count, tok_rows, KV_HEADS, group, HEAD_DIM)
    g5 = grad_out.reshape(seq_count, tok_rows, KV_HEADS, group, HEAD_DIM)
    o5 = outputs.reshape(seq_count, tok_rows, KV_HEADS, group, HEAD_DIM)
    delta_rows = jnp.sum(o5.astype(jnp.float32) * g5.astype(jnp.float32), axis=4)
    delta_heads = jnp.transpose(delta_rows, (0, 2, 3, 1))
    lse_heads = jnp.transpose(
        lse_rows.reshape(seq_count, tok_rows, KV_HEADS, group), (0, 2, 3, 1)
    )
    query_pos = shard_positions(here)

    def block_grads(kv_blk, key_pos):
        keys_here = kv_blk[0].reshape(seq_count, tok_rows, KV_HEADS, HEAD_DIM)
        values_here = kv_blk[1].reshape(seq_count, tok_rows, KV_HEADS, HEAD_DIM)
        scores = jnp.einsum(
            "sqgrd,skgd->sgrqk", q5, keys_here, preferred_element_type=jnp.float32
        )
        allowed = key_pos[None, :] <= query_pos[:, None]
        attn_probs = jnp.exp(
            jnp.where(allowed, scores * score_scale - lse_heads[..., None], -jnp.inf)
        )
        dprobs = jnp.einsum(
            "sqgrd,skgd->sgrqk", g5, values_here, preferred_element_type=jnp.float32
        )
        dscores = (attn_probs * (dprobs - delta_heads[..., None])).astype(jnp.bfloat16)
        query_part = jnp.einsum(
            "sgrqk,skgd->sqgrd", dscores, keys_here, preferred_element_type=jnp.float32
        )
        key_part = (
            jnp.einsum("sgrqk,sqgrd->skgd", dscores, q5, preferred_element_type=jnp.float32)
            * score_scale
        )
        value_part = jnp.einsum(
            "sgrqk,sqgrd->skgd",
            attn_probs.astype(jnp.bfloat16),
            g5,
            preferred_element_type=jnp.float32,
        )
        flat = (seq_count, tok_rows, KV_HEADS * HEAD_DIM)
        return query_part, key_part.reshape(flat), value_part.reshape(flat)

    query_sum, key_sum, value_sum = block_grads(own_kv, query_pos)
    for step in range(1, CYCLE_STEPS):
        source = (here - step) % cycle_size
        part_query, part_key, part_value = block_grads(kv_ahead[step - 1], shard_positions(source))
        query_sum = query_sum + part_query
        returned = passed_along(
            jnp.stack((part_key, part_value)).astype(jnp.bfloat16), "ctx", -step
        )
        key_sum = key_sum + returned[0].astype(jnp.float32)
        value_sum = value_sum + returned[1].astype(jnp.float32)
    query_grad = (query_sum * score_scale).astype(jnp.bfloat16).reshape(query.shape)
    return (query_grad, key_sum.astype(jnp.bfloat16), value_sum.astype(jnp.bfloat16))


def solution(mesh):
    in_specs = (
        P("head", "ctx", None),
        P("head", "ctx", None),
        P("head", "ctx", None),
        P(None, "ctx", "head"),
        P("head", "ctx", None),
        P(None, "ctx", "head"),
        P(),
    )
    out_specs = (P("head", "ctx", None), P("head", "ctx", None), P("head", "ctx", None))
    return jax.shard_map(shards, mesh=mesh, in_specs=in_specs, out_specs=out_specs, check_vma=False)
```

time: 255 us -> 96 us (0.38)
  the two profiles are of different devices: /device:TPU:78 before, /device:TPU:118 now
where the time goes in v1:
time: 96 us; the launch traced here: 95.4 us
  starting transfers between devices  43.9 us (46%)
  waiting for transfers between devices  22.7 us (24%)
  local copies, waits for them, and re-layouts  12.3 us (13%)
  matrix products  8.15 us (8%)
  other arithmetic  7.5 us (8%)
  between operations  0.96 us (1%)
    all_to_all x1, starting transfers between devices, shards(): lax.all_to_all(logsumexp, 'head', split_axis=0, concat_axis=2, tiled=True)  22.1 us
    ppermute x4, starting transfers between devices, passed_along(): return lax.ppermute(value, axis, pairs)  12.5 us
    ppermute x4, waiting for transfers between devices, passed_along(): return lax.ppermute(value, axis, pairs)  11.4 us
    all_to_all x1, starting transfers between devices, shards(): lax.all_to_all(attn_out, 'head', split_axis=0, concat_axis=2, tiled=True)  9.31 us
    all_to_all x1, waiting for transfers between devices, shards(): lax.all_to_all(attn_out, 'head', split_axis=0, concat_axis=2, tiled=True)  7.52 us
    unnamed x37, local copies, waits for them, and re-layouts  4 us
    all_to_all x1, waiting for transfers between devices, shards(): lax.all_to_all(logsumexp, 'head', split_axis=0, concat_axis=2, tiled=True)  3.72 us
    another operation x4, local copies, waits for them, and re-layouts, shards(): jnp.stack((part_key, part_value)).astype(jnp.bfloat16)  3.33 us
  transfers between devices with their start and end apart: 6, of which 4 were waited for; matrix products, arithmetic and copies ran while one was open for 14% of the time, Pallas kernels for 0%

profile of v1, /device:TPU:118, one launch (start us, length us, event | category | flops | bytes accessed | tf_op | source)
XLA Modules:
  0.0 95.4 jit_solution(12595817712071511392)
XLA Ops:
  0.6 1.1 %copy.51 = bf16[1,128,512]{1,2,0:T(8,128)(2,1)S(1)} copy(bf16[1,128,512]{2,1,0:T(8,128)(2,1)} %param.8) | data formatting | bytes 262144 | tf_op args[1]
  1.9 0.7 pad_maximum_fusion
  2.6 2.0 %collective-permute-start = (bf16[2,1,128,512]{2,3,1,0:T(8,128)(2,1)}, bf16[2,1,128,512]{2,3,1,0:T(8,128)(2,1)S(1)}, u32[]{:S(2)}, u32[]{:S(2)}) collective-permute-start(bf16[2,1,128,512]{2,3,1,0:T(8,128)(2,1)} %pad_maximum_fusion), channel_id=1, source_target_pairs={{0,16},{16,32},{32,48},{48,64},{64,80},{80,96},{96,112},{112,128},... | collective-permute-start | bytes 786440 | tf_op jit(solution)/shard_map/ppermute | solution.py:15
  4.6 6.6 %collective-permute-start.1 = (bf16[2,1,128,512]{2,3,1,0:T(8,128)(2,1)}, bf16[2,1,128,512]{2,3,1,0:T(8,128)(2,1)}, u32[]{:S(2)}, u32[]{:S(2)}) collective-permute-start(bf16[2,1,128,512]{2,3,1,0:T(8,128)(2,1)} %pad_maximum_fusion), channel_id=1, source_target_pairs={{0,32},{16,48},{32,64},{48,80},{64,96},{80,112},{96,128},{112,144}... | collective-permute-start | bytes 786440 | tf_op jit(solution)/shard_map/ppermute | solution.py:15
  11.3 22.1 %all-to-all-start = ((f32[16,128,1]{1,2,0:T(1,128)}), f32[16,128,1]{1,2,0:T(1,128)S(1)}, u32[]{:S(2)}, u32[]{:S(2)}) async-start(f32[16,128,1]{1,2,0:T(1,128)} %param.12), calls=%async_computation | async-start | bytes 16384 | tf_op jit(solution)/shard_map/all_to_all | solution.py:36
  33.8 0.7 broadcast_compare_fusion.1
  34.6 0.7 reshape.405
  35.5 0.8 copy-done.4
  36.7 3.7 %all-to-all-done = f32[16,128,1]{1,2,0:T(1,128)S(1)} async-done(((f32[16,128,1]{1,2,0:T(1,128)}), f32[16,128,1]{1,2,0:T(1,128)S(1)}, u32[]{:S(2)}, u32[]{:S(2)}) %all-to-all-start) | async-done | bytes 8224 | tf_op jit(solution)/shard_map/all_to_all | solution.py:36
  40.5 9.3 %all-to-all-start.1 = ((bf16[16,128,128]{2,1,0:T(8,128)(2,1)}), bf16[16,128,128]{2,1,0:T(8,128)(2,1)}, u32[]{:S(2)}, u32[]{:S(2)}) async-start(bf16[16,128,128]{2,1,0:T(8,128)(2,1)} %param.10), calls=%async_computation.1 | async-start | bytes 1048576 | tf_op jit(solution)/shard_map/all_to_all | solution.py:35
  49.8 0.4 fusion.13
  50.5 0.8 copy.80
  51.3 0.7 fusion.45
  52.7 0.8 copy.70
  53.5 1.7 %fusion.46 = (bf16[1,1,128,512]{2,3,1,0:T(8,128)(2,1)}, bf16[1,1,128,512]{2,3,1,0:T(8,128)(2,1)S(1)}) fusion(bf16[2,1,128,512]{2,3,1,0:T(8,128)(2,1)} %collective-permute-done.1), kind=kLoop, calls=%fused_computation.82 | loop fusion | bytes 524288 | tf_op jit(solution)/shard_map/slice | solution.py:50
  55.1 0.4 fusion.19
  55.5 0.9 copy-done
  56.5 1.0 %fusion.33 = bf16[4,128,128]{1,2,0:T(8,128)(2,1)} fusion(bf16[128,4,4,128]{0,3,2,1:T(8,128)(2,1)S(1)} %bitcast.277, f32[1,4,4,128,128]{3,4,2,1,0:T(8,128)S(1)} %fusion.19), kind=kOutput, calls=%fused_computation.46 | convolution fusion | flops 67436544 | bytes 1703936 | tf_op jit(solution)/shard_map/sgrqk,sqgrd->skgd/dot_general | solution.py:69
  57.4 1.7 %copy.77 = bf16[1,1,128,512]{3,2,1,0:T(8,128)(2,1)} copy(bf16[1,1,128,512]{2,3,1,0:T(8,128)(2,1)} %bitcast.297) | data formatting | bytes 262144 | tf_op jit(solution)/shard_map/stack | solution.py:84
  59.1 7.5 %all-to-all-done.1 = bf16[16,128,128]{2,1,0:T(8,128)(2,1)} async-done(((bf16[16,128,128]{2,1,0:T(8,128)(2,1)}), bf16[16,128,128]{2,1,0:T(8,128)(2,1)}, u32[]{:S(2)}, u32[]{:S(2)}) %all-to-all-start.1) | async-done | bytes 524320 | tf_op jit(solution)/shard_map/all_to_all | solution.py:35
  66.6 1.6 %fusion.34 = f32[128,16]{0,1:T(8,128)S(1)} fusion(bf16[16,128,128]{2,1,0:T(8,128)(2,1)} %all-to-all-done.1, bf16[1,128,2048]{2,1,0:T(8,128)(2,1)} %param.11), kind=kLoop, calls=%fused_computation.48 | loop fusion | flops 1046528 | bytes 1056768 | tf_op jit(solution)/shard_map/reduce_sum | solution.py:41
  68.5 1.0 %fusion.27 = f32[4,128,128]{1,2,0:T(8,128)} fusion(bf16[4,4,128,128]{2,3,1,0:T(8,128)(2,1)S(1)} %fusion.24, bf16[128,4,4,128]{0,3,2,1:T(8,128)(2,1)S(1)} %bitcast.272), kind=kOutput, calls=%fused_computation.40 | convolution fusion | flops 67174400 | bytes 1310720 | tf_op jit(solution)/shard_map/sgrqk,sqgrd->skgd/dot_general | solution.py:66
  69.5 1.3 %convolution_bitcast_fusion = f32[4,128,4,128]{3,1,2,0:T(8,128)} fusion(bf16[128,4,128,1]{0,2,3,1:T(8,128)(2,1)S(1)} %copy.85, bf16[4,4,128,128]{2,3,1,0:T(8,128)(2,1)S(1)} %fusion.24), kind=kOutput, calls=%fused_computation | convolution fusion | flops 67108864 | bytes 1703936 | tf_op jit(solution)/shard_map/sgrqk,skgd->sqgrd/dot_general | solution.py:62
  71.6 1.2 %fusion.47 = f32[4,128,4,128]{3,1,2,0:T(8,128)} fusion(bf16[128,4,128,1]{0,2,3,1:T(8,128)(2,1)S(1)} %bitcast.285, bf16[4,4,128,128]{2,3,1,0:T(8,128)(2,1)S(1)} %fusion.26), kind=kOutput, calls=%fused_computation.83 | convolution fusion | flops 67108864 | bytes 1703936 | tf_op jit(solution)/shard_map/sgrqk,skgd->sqgrd/dot_general | solution.py:62
  73.5 0.8 copy.69
  74.3 1.6 %pad_maximum_fusion.1 = bf16[2,1,128,512]{3,2,1,0:T(8,128)(2,1)} fusion(bf16[1,1,128,512]{3,2,1,0:T(8,128)(2,1)S(1)} %copy-done.13, bf16[1,1,128,512]{3,2,1,0:T(8,128)(2,1)} %copy.69), kind=kLoop, calls=%fused_computation.59 | loop fusion | flops 131072 | bytes 524288 | tf_op jit(solution)/shard_map/stack | solution.py:84
  75.9 1.9 %collective-permute-start.2 = (bf16[2,1,128,512]{3,2,1,0:T(8,128)(2,1)}, bf16[2,1,128,512]{3,2,1,0:T(8,128)(2,1)}, u32[]{:S(2)}, u32[]{:S(2)}) collective-permute-start(bf16[2,1,128,512]{3,2,1,0:T(8,128)(2,1)} %pad_maximum_fusion.1), channel_id=1, source_target_pairs={{0,1008},{16,0},{32,16},{48,32},{64,48},{80,64},{96,80},{112,96},{... | collective-permute-start | bytes 786440 | tf_op jit(solution)/shard_map/ppermute | solution.py:15
  78.0 0.7 pad_maximum_fusion.2
  78.7 1.9 %collective-permute-start.3 = (bf16[2,1,128,512]{3,2,1,0:T(8,128)(2,1)}, bf16[2,1,128,512]{3,2,1,0:T(8,128)(2,1)}, u32[]{:S(2)}, u32[]{:S(2)}) collective-permute-start(bf16[2,1,128,512]{3,2,1,0:T(8,128)(2,1)} %pad_maximum_fusion.2), channel_id=1, source_target_pairs={{0,992},{16,1008},{32,0},{48,16},{64,32},{80,48},{96,64},{112,80},... | collective-permute-start | bytes 786440 | tf_op jit(solution)/shard_map/ppermute | solution.py:15
  81.1 1.0 %copy.81 = bf16[1,128,2048]{2,1,0:T(8,128)(2,1)} copy(bf16[1,128,2048]{1,2,0:T(8,128)(2,1)S(1)} %bitcast.281) | data formatting | bytes 1048576
  82.2 11.3 %collective-permute-done.3 = bf16[2,1,128,512]{3,2,1,0:T(8,128)(2,1)} collective-permute-done((bf16[2,1,128,512]{3,2,1,0:T(8,128)(2,1)}, bf16[2,1,128,512]{3,2,1,0:T(8,128)(2,1)}, u32[]{:S(2)}, u32[]{:S(2)}) %collective-permute-start.3) | collective-permute-done | bytes 262176 | tf_op jit(solution)/shard_map/ppermute | solution.py:15
  93.5 1.9 %fusion.42 = (bf16[1,128,512]{2,1,0:T(8,128)(2,1)}, bf16[1,128,512]{2,1,0:T(8,128)(2,1)}) fusion(f32[1,128,512]{2,1,0:T(8,128)S(1)} %copy-done.5, bf16[2,1,128,512]{3,2,1,0:T(8,128)(2,1)} %collective-permute-done.3, bf16[2,1,128,512]{3,2,1,0:T(8,128)(2,1)} %collective-permute-done.2, f32[1,128,512]{2,1,0:T(8,128)S(1)} %copy.71), kind=kLoop, calls=%fused_computation.62 | loop fusion | flops 655360 | bytes 1310720 | tf_op jit(solution)/shard_map/convert_element_type | solution.py:89
  (57 shorter events, 4.6 us)
Async XLA Ops:
  0.6 1.1 %copy-start.10 = (bf16[1,128,512]{2,1,0:T(8,128)(2,1)S(1)}, bf16[1,128,512]{2,1,0:T(8,128)(2,1)}, u32[]{:S(2)}) copy-start(bf16[1,128,512]{2,1,0:T(8,128)(2,1)} %param.9) | copy-start | bytes 393220
  1.8 31.5 %copy-start.16 = (s32[128]{0:T(128)S(1)}, s32[128]{0:T(128)}, u32[]{:S(2)}) copy-start(s32[128]{0:T(128)} %param.13) | copy-start | bytes 1540
  1.8 33.4 %copy-start.8 = (bf16[1,128,2048]{2,1,0:T(8,128)(2,1)S(1)}, bf16[1,128,2048]{2,1,0:T(8,128)(2,1)}, u32[]{:S(2)}) copy-start(bf16[1,128,2048]{2,1,0:T(8,128)(2,1)} %param.7) | copy-start | bytes 1572868
  2.6 32.0 %copy-start.9 = (bf16[1,128,512]{2,1,0:T(8,128)(2,1)S(1)}, bf16[1,128,512]{2,1,0:T(8,128)(2,1)}, u32[]{:S(2)}) copy-start(bf16[1,128,512]{2,1,0:T(8,128)(2,1)} %param.8) | copy-start | bytes 393220
  2.6 48.7 %collective-permute-start = (bf16[2,1,128,512]{2,3,1,0:T(8,128)(2,1)}, bf16[2,1,128,512]{2,3,1,0:T(8,128)(2,1)S(1)}, u32[]{:S(2)}, u32[]{:S(2)}) collective-permute-start(bf16[2,1,128,512]{2,3,1,0:T(8,128)(2,1)} %pad_maximum_fusion), channel_id=1, source_target_pairs={{0,16},{16,32},{32,48},{48,64},{64,80},{80,96},{96,112},{112,128},... | collective-permute-start | bytes 786440 | tf_op jit(solution)/shard_map/ppermute | solution.py:15
  4.6 48.8 %collective-permute-start.1 = (bf16[2,1,128,512]{2,3,1,0:T(8,128)(2,1)}, bf16[2,1,128,512]{2,3,1,0:T(8,128)(2,1)}, u32[]{:S(2)}, u32[]{:S(2)}) collective-permute-start(bf16[2,1,128,512]{2,3,1,0:T(8,128)(2,1)} %pad_maximum_fusion), channel_id=1, source_target_pairs={{0,32},{16,48},{32,64},{48,80},{64,96},{80,112},{96,128},{112,144}... | collective-permute-start | bytes 786440 | tf_op jit(solution)/shard_map/ppermute | solution.py:15
  11.3 29.2 %all-to-all-start = ((f32[16,128,1]{1,2,0:T(1,128)}), f32[16,128,1]{1,2,0:T(1,128)S(1)}, u32[]{:S(2)}, u32[]{:S(2)}) async-start(f32[16,128,1]{1,2,0:T(1,128)} %param.12), calls=%async_computation | async-start | bytes 16384 | tf_op jit(solution)/shard_map/all_to_all | solution.py:36
  35.3 1.0 %copy-start.4 = (bf16[1,128,2048]{2,1,0:T(8,128)(2,1)S(1)}, bf16[1,128,2048]{2,1,0:T(8,128)(2,1)}, u32[]{:S(2)}) copy-start(bf16[1,128,2048]{2,1,0:T(8,128)(2,1)} %param.11) | copy-start | bytes 1572868
  40.5 26.2 %all-to-all-start.1 = ((bf16[16,128,128]{2,1,0:T(8,128)(2,1)}), bf16[16,128,128]{2,1,0:T(8,128)(2,1)}, u32[]{:S(2)}, u32[]{:S(2)}) async-start(bf16[16,128,128]{2,1,0:T(8,128)(2,1)} %param.10), calls=%async_computation.1 | async-start | bytes 1048576 | tf_op jit(solution)/shard_map/all_to_all | solution.py:35
  53.5 1.7 %copy-start.15 = (pred[128,128]{0,1:T(8,128)(4,1)S(1)}, pred[128,128]{0,1:T(8,128)(4,1)}, u32[]{:S(2)}) copy-start(pred[128,128]{0,1:T(8,128)(4,1)} %get-tuple-element.16) | copy-start | bytes 49156
  55.5 1.0 %copy-start = (f32[1,4,4,128,128]{3,4,2,1,0:T(8,128)}, f32[1,4,4,128,128]{3,4,2,1,0:T(8,128)S(1)}, u32[]{:S(2)}) copy-start(f32[1,4,4,128,128]{3,4,2,1,0:T(8,128)S(1)} %fusion.19) | copy-start | bytes 3145732
  66.6 1.6 %copy-start.7 = (bf16[128,4,128]{2,1,0:T(4,128)(2,1)S(1)}, bf16[128,4,128]{2,1,0:T(4,128)(2,1)}, u32[]{:S(2)}) copy-start(bf16[128,4,128]{2,1,0:T(4,128)(2,1)} %reshape.405) | copy-start | bytes 393220
  69.5 1.3 %copy-start.1 = (f32[1,4,4,128,128]{3,4,2,1,0:T(8,128)S(1)}, f32[1,4,4,128,128]{3,4,2,1,0:T(8,128)}, u32[]{:S(2)}) copy-start(f32[1,4,4,128,128]{3,4,2,1,0:T(8,128)} %copy-done) | copy-start | bytes 3145732
  69.5 1.3 %copy-start.12 = (bf16[1,1,128,512]{2,3,1,0:T(8,128)(2,1)S(1)}, bf16[1,1,128,512]{2,3,1,0:T(8,128)(2,1)}, u32[]{:S(2)}) copy-start(bf16[1,1,128,512]{2,3,1,0:T(8,128)(2,1)} %get-tuple-element.13) | copy-start | bytes 393220
  71.5 1.3 %copy-start.11 = (bf16[1,1,128,512]{2,3,1,0:T(8,128)(2,1)S(1)}, bf16[1,1,128,512]{2,3,1,0:T(8,128)(2,1)}, u32[]{:S(2)}) copy-start(bf16[1,1,128,512]{2,3,1,0:T(8,128)(2,1)} %get-tuple-element.11) | copy-start | bytes 393220
  73.2 1.1 %copy-start.13 = (bf16[1,1,128,512]{3,2,1,0:T(8,128)(2,1)S(1)}, bf16[1,1,128,512]{3,2,1,0:T(8,128)(2,1)}, u32[]{:S(2)}) copy-start(bf16[1,1,128,512]{3,2,1,0:T(8,128)(2,1)} %copy.70) | copy-start | bytes 393220
  73.2 4.8 %copy-start.14 = (bf16[1,1,128,512]{3,2,1,0:T(8,128)(2,1)S(1)}, bf16[1,1,128,512]{3,2,1,0:T(8,128)(2,1)}, u32[]{:S(2)}) copy-start(bf16[1,1,128,512]{3,2,1,0:T(8,128)(2,1)} %copy.77) | copy-start | bytes 393220
  73.2 7.5 %copy-start.6 = (f32[4,128,128]{1,2,0:T(8,128)S(1)}, f32[4,128,128]{1,2,0:T(8,128)}, u32[]{:S(2)}) copy-start(f32[4,128,128]{1,2,0:T(8,128)} %fusion.27) | copy-start | bytes 786436
  73.5 7.3 %copy-start.2 = (f32[4,128,4,128]{3,1,2,0:T(8,128)S(1)}, f32[4,128,4,128]{3,1,2,0:T(8,128)}, u32[]{:S(2)}) copy-start(f32[4,128,4,128]{3,1,2,0:T(8,128)} %convolution_bitcast_fusion) | copy-start | bytes 3145732
  73.5 7.3 %copy-start.3 = (f32[4,128,4,128]{3,1,2,0:T(8,128)S(1)}, f32[4,128,4,128]{3,1,2,0:T(8,128)}, u32[]{:S(2)}) copy-start(f32[4,128,4,128]{3,1,2,0:T(8,128)} %fusion.47) | copy-start | bytes 3145732
  75.9 6.3 %collective-permute-start.2 = (bf16[2,1,128,512]{3,2,1,0:T(8,128)(2,1)}, bf16[2,1,128,512]{3,2,1,0:T(8,128)(2,1)}, u32[]{:S(2)}, u32[]{:S(2)}) collective-permute-start(bf16[2,1,128,512]{3,2,1,0:T(8,128)(2,1)} %pad_maximum_fusion.1), channel_id=1, source_target_pairs={{0,1008},{16,0},{32,16},{48,32},{64,48},{80,64},{96,80},{112,96},{... | collective-permute-start | bytes 786440 | tf_op jit(solution)/shard_map/ppermute | solution.py:15
  78.7 14.8 %collective-permute-start.3 = (bf16[2,1,128,512]{3,2,1,0:T(8,128)(2,1)}, bf16[2,1,128,512]{3,2,1,0:T(8,128)(2,1)}, u32[]{:S(2)}, u32[]{:S(2)}) collective-permute-start(bf16[2,1,128,512]{3,2,1,0:T(8,128)(2,1)} %pad_maximum_fusion.2), channel_id=1, source_target_pairs={{0,992},{16,1008},{32,0},{48,16},{64,32},{80,48},{96,64},{112,80},... | collective-permute-start | bytes 786440 | tf_op jit(solution)/shard_map/ppermute | solution.py:15
  81.1 12.4 %copy-start.5 = (f32[1,128,512]{2,1,0:T(8,128)S(1)}, f32[1,128,512]{2,1,0:T(8,128)}, u32[]{:S(2)}) copy-start(f32[1,128,512]{2,1,0:T(8,128)} %copy.80) | copy-start | bytes 786436

commit v2 on v1

--- a/solution.py
+++ b/solution.py
@@ -32,17 +32,27 @@
     own_kv = jnp.stack((key, value))
     kv_ahead = [passed_along(own_kv, "ctx", step) for step in range(1, CYCLE_STEPS)]
 
-    outputs = lax.all_to_all(attn_out, "head", split_axis=0, concat_axis=2, tiled=True)
-    lse_rows = lax.all_to_all(logsumexp, "head", split_axis=0, concat_axis=2, tiled=True)
+    lse_t = jnp.transpose(logsumexp, (0, 2, 1)).reshape(logsumexp.shape[0], 1, -1)
+    lse_hi = lax.reduce_precision(lse_t, exponent_bits=8, mantissa_bits=7)
+    lse_r1 = lse_t - lse_hi
+    lse_mid = lax.reduce_precision(lse_r1, exponent_bits=8, mantissa_bits=7)
+    lse_lo = lse_r1 - lse_mid
+    packed = jnp.concatenate(
+        (attn_out, lse_hi.astype(jnp.bfloat16), lse_mid.astype(jnp.bfloat16),
+         lse_lo.astype(jnp.bfloat16)),
+        axis=1,
+    )
+    moved = lax.all_to_all(packed, "head", split_axis=0, concat_axis=2, tiled=True)
+    outputs = moved[:, :tok_rows, :]
+    lse_parts = moved[:, tok_rows:, :].astype(jnp.float32)
+    lse_sum = (lse_parts[:, 0] + lse_parts[:, 1]) + lse_parts[:, 2]
 
     q5 = query.reshape(seq_count, tok_rows, KV_HEADS, group, HEAD_DIM)
     g5 = grad_out.reshape(seq_count, tok_rows, KV_HEADS, group, HEAD_DIM)
     o5 = outputs.reshape(seq_count, tok_rows, KV_HEADS, group, HEAD_DIM)
     delta_rows = jnp.sum(o5.astype(jnp.float32) * g5.astype(jnp.float32), axis=4)
     delta_heads = jnp.transpose(delta_rows, (0, 2, 3, 1))
-    lse_heads = jnp.transpose(
-        lse_rows.reshape(seq_count, tok_rows, KV_HEADS, group), (0, 2, 3, 1)
-    )
+    lse_heads = lse_sum.reshape(seq_count, KV_HEADS, group, tok_rows)
     query_pos = shard_positions(here)
 
     def block_grads(kv_blk, key_pos):

time: 96 us -> 90.1 us (0.939)
  starting transfers between devices: 43.9 us -> 34.6 us
  waiting for transfers between devices: 22.7 us -> 25.5 us
  local copies, waits for them, and re-layouts: 12.3 us -> 13.7 us
  matrix products: 8.15 us -> 7.18 us
    all_to_all x2 -> x1, starting transfers between devices: 31.4 us -> 22.2 us  [shards(): lax.all_to_all(packed, 'head', split_axis=0, concat_axis=2, tiled=True)]
    all_to_all x2 -> x1, waiting for transfers between devices: 11.2 us -> 15.6 us  [shards(): lax.all_to_all(packed, 'head', split_axis=0, concat_axis=2, tiled=True)]
    ppermute x4, waiting for transfers between devices: 11.4 us -> 9.89 us  [passed_along(): return lax.ppermute(value, axis, pairs)]
    another operation x4, local copies, waits for them, and re-layouts: 3.33 us -> 2 us  [shards(): jnp.stack((part_key, part_value)).astype(jnp.bfloat16)]
    mul x0 -> x1, other arithmetic: none -> 1.16 us  [shards(): o5.astype(jnp.float32) * g5.astype(jnp.float32)]
    dot_general x3, matrix products: 2.84 us -> 1.88 us  [block_grads(): jnp.einsum('sgrqk,skgd->sqgrd', dscores, keys_here, preferred_element_typ...]
    unnamed x37 -> x33, local copies, waits for them, and re-layouts: 4 us -> 4.85 us
  transfers between devices with their start and end apart: 6 -> 5, of which waited for: 4 -> 2; matrix products, arithmetic and copies ran while one was open for 14% -> 13% of each run, Pallas kernels for 0% -> 0%
where the time goes in v2:
time: 90.1 us; the launch traced here: 89.5 us
  starting transfers between devices  34.6 us (38%)
  waiting for transfers between devices  25.5 us (28%)
  local copies, waits for them, and re-layouts  13.7 us (15%)
  other arithmetic  7.52 us (8%)
  matrix products  7.18 us (8%)
  between operations  1.13 us (1%)
    all_to_all x1, starting transfers between devices, shards(): lax.all_to_all(packed, 'head', split_axis=0, concat_axis=2, tiled=True)  22.2 us
    all_to_all x1, waiting for transfers between devices, shards(): lax.all_to_all(packed, 'head', split_axis=0, concat_axis=2, tiled=True)  15.6 us
    ppermute x4, starting transfers between devices, passed_along(): return lax.ppermute(value, axis, pairs)  12.4 us
    ppermute x4, waiting for transfers between devices, passed_along(): return lax.ppermute(value, axis, pairs)  9.89 us
    unnamed x33, local copies, waits for them, and re-layouts  4.85 us
    another operation x2, other arithmetic, shards(): jnp.stack((part_key, part_value)).astype(jnp.bfloat16)  2.36 us
    slice x2, local copies, waits for them, and re-layouts, block_grads(): values_here = kv_blk[1].reshape(seq_count, tok_rows, KV_HEADS, HEAD_DIM)  2.35 us
    dot_general x3, matrix products, block_grads(): jnp.einsum('sgrqk,sqgrd->skgd', attn_probs.astype(jnp.bfloat16), g5, pref...  2.2 us
  transfers between devices with their start and end apart: 5, of which 2 were waited for; matrix products, arithmetic and copies ran while one was open for 13% of the time, Pallas kernels for 0%

profile of v2, /device:TPU:118, one launch (start us, length us, event | category | flops | bytes accessed | tf_op | source)
XLA Modules:
  0.0 89.5 jit_solution(14231692492600081369)
XLA Ops:
  0.7 1.1 %copy.99 = bf16[1,128,512]{1,2,0:T(8,128)(2,1)S(1)} copy(bf16[1,128,512]{2,1,0:T(8,128)(2,1)} %param.8) | data formatting | bytes 262144 | tf_op args[1]
  1.7 1.0 %copy.100 = bf16[1,128,512]{1,2,0:T(8,128)(2,1)S(1)} copy(bf16[1,128,512]{2,1,0:T(8,128)(2,1)} %param.9) | data formatting | bytes 262144 | tf_op args[2]
  2.8 1.9 %collective-permute-start = (bf16[2,1,128,512]{2,3,1,0:T(8,128)(2,1)S(1)}, bf16[2,1,128,512]{2,3,1,0:T(8,128)(2,1)}, u32[]{:S(2)}, u32[]{:S(2)}) collective-permute-start(bf16[2,1,128,512]{2,3,1,0:T(8,128)(2,1)S(1)} %pad_maximum_fusion.1), channel_id=1, source_target_pairs={{0,16},{16,32},{32,48},{48,64},{64,80},{80,96},{96,112},{112,128},... | collective-permute-start | bytes 786440 | tf_op jit(solution)/shard_map/ppermute | solution.py:15
  4.7 6.6 %collective-permute-start.1 = (bf16[2,1,128,512]{2,3,1,0:T(8,128)(2,1)S(1)}, bf16[2,1,128,512]{2,3,1,0:T(8,128)(2,1)S(1)}, u32[]{:S(2)}, u32[]{:S(2)}) collective-permute-start(bf16[2,1,128,512]{2,3,1,0:T(8,128)(2,1)S(1)} %pad_maximum_fusion.1), channel_id=1, source_target_pairs={{0,32},{16,48},{32,64},{48,80},{64,96},{80,112},{96,128},{112,144}... | collective-permute-start | bytes 786440 | tf_op jit(solution)/shard_map/ppermute | solution.py:15
  11.5 0.9 pad_maximum_fusion
  12.4 22.2 %all-to-all-start = ((bf16[16,131,128]{2,1,0:T(8,128)(2,1)}), bf16[16,131,128]{2,1,0:T(8,128)(2,1)S(1)}, u32[]{:S(2)}, u32[]{:S(2)}) async-start(bf16[16,131,128]{2,1,0:T(8,128)(2,1)} %pad_maximum_fusion), calls=%async_computation | async-start | bytes 1114112 | tf_op jit(solution)/shard_map/all_to_all | solution.py:45
  35.3 0.7 reshape.487
  36.7 1.6 %fusion.45 = (bf16[1,1,128,512]{2,3,1,0:T(8,128)(2,1)}, bf16[1,1,128,512]{2,3,1,0:T(8,128)(2,1)S(1)}) fusion(bf16[2,1,128,512]{2,3,1,0:T(8,128)(2,1)} %collective-permute-done), kind=kLoop, calls=%fused_computation.87 | loop fusion | bytes 524288 | tf_op jit(solution)/shard_map/slice | solution.py:60
  38.3 0.7 fusion.46
  39.1 15.6 %all-to-all-done = bf16[16,131,128]{2,1,0:T(8,128)(2,1)S(1)} async-done(((bf16[16,131,128]{2,1,0:T(8,128)(2,1)}), bf16[16,131,128]{2,1,0:T(8,128)(2,1)S(1)}, u32[]{:S(2)}, u32[]{:S(2)}) %all-to-all-start) | async-done | bytes 536608 | tf_op jit(solution)/shard_map/all_to_all | solution.py:45
  55.0 1.2 %convert_multiply_fusion = f32[1,128,2048]{2,1,0:T(8,128)S(1)} fusion(bf16[1,128,2048]{2,1,0:T(8,128)(2,1)} %param.11, bf16[1,131,2048]{2,1,0:T(8,128)(2,1)S(1)} %all_to_all.16), kind=kLoop, calls=%fused_computation.47 | loop fusion | flops 786432 | bytes 2097152 | tf_op jit(solution)/shard_map/mul | solution.py:53
  56.2 0.7 mul.123
  56.9 0.8 reduce_sum.11
  57.8 0.4 fusion.13
  58.6 0.6 copy-done.5
  60.1 0.6 copy-done.2
  61.1 1.0 %fusion.33 = bf16[4,128,128]{1,2,0:T(8,128)(2,1)} fusion(bf16[128,4,4,128]{0,3,2,1:T(8,128)(2,1)S(1)} %bitcast.261, f32[1,4,4,128,128]{3,4,2,1,0:T(8,128)S(1)} %fusion.19), kind=kOutput, calls=%fused_computation.46 | convolution fusion | flops 67436544 | bytes 1703936 | tf_op jit(solution)/shard_map/sgrqk,sqgrd->skgd/dot_general | solution.py:79
  62.7 1.3 %fusion.47 = f32[4,128,4,128]{3,1,2,0:T(8,128)} fusion(bf16[128,4,128,1]{0,2,3,1:T(8,128)(2,1)S(1)} %bitcast.270, bf16[4,4,128,128]{2,3,1,0:T(8,128)(2,1)S(1)} %fusion.26), kind=kOutput, calls=%fused_computation.89 | convolution fusion | flops 67108864 | bytes 1703936 | tf_op jit(solution)/shard_map/sgrqk,skgd->sqgrd/dot_general | solution.py:72
  64.0 0.4 fusion.16
  64.4 1.0 %fusion.32 = bf16[4,128,128]{1,2,0:T(8,128)(2,1)} fusion(bf16[128,4,4,128]{0,3,2,1:T(8,128)(2,1)S(1)} %bitcast.263, f32[1,4,4,128,128]{3,4,2,1,0:T(8,128)S(1)} %fusion.16), kind=kOutput, calls=%fused_computation.45 | convolution fusion | flops 67436544 | bytes 1703936 | tf_op jit(solution)/shard_map/sgrqk,sqgrd->skgd/dot_general | solution.py:79
  66.2 0.5 copy-done.12
  66.8 0.7 pad_maximum_fusion.2
  67.5 1.9 %collective-permute-start.2 = (bf16[2,1,128,512]{3,2,1,0:T(8,128)(2,1)}, bf16[2,1,128,512]{3,2,1,0:T(8,128)(2,1)}, u32[]{:S(2)}, u32[]{:S(2)}) collective-permute-start(bf16[2,1,128,512]{3,2,1,0:T(8,128)(2,1)} %pad_maximum_fusion.2), channel_id=1, source_target_pairs={{0,1008},{16,0},{32,16},{48,32},{64,48},{80,64},{96,80},{112,96},{... | collective-permute-start | bytes 786440 | tf_op jit(solution)/shard_map/ppermute | solution.py:15
  69.4 0.8 copy.124
  70.2 1.0 %copy.125 = bf16[1,1,128,512]{3,2,1,0:T(8,128)(2,1)S(1)} copy(bf16[1,1,128,512]{2,3,1,0:T(8,128)(2,1)} %bitcast.282) | data formatting | bytes 262144 | tf_op jit(solution)/shard_map/stack | solution.py:94
  71.2 1.6 %pad_maximum_fusion.3 = bf16[2,1,128,512]{3,2,1,0:T(8,128)(2,1)} fusion(bf16[1,1,128,512]{3,2,1,0:T(8,128)(2,1)S(1)} %copy.125, bf16[1,1,128,512]{3,2,1,0:T(8,128)(2,1)} %copy.124), kind=kLoop, calls=%fused_computation.58 | loop fusion | flops 131072 | bytes 524288 | tf_op jit(solution)/shard_map/stack | solution.py:94
  72.8 1.9 %collective-permute-start.3 = (bf16[2,1,128,512]{3,2,1,0:T(8,128)(2,1)}, bf16[2,1,128,512]{3,2,1,0:T(8,128)(2,1)}, u32[]{:S(2)}, u32[]{:S(2)}) collective-permute-start(bf16[2,1,128,512]{3,2,1,0:T(8,128)(2,1)} %pad_maximum_fusion.3), channel_id=1, source_target_pairs={{0,992},{16,1008},{32,0},{48,16},{64,32},{80,48},{96,64},{112,80},... | collective-permute-start | bytes 786440 | tf_op jit(solution)/shard_map/ppermute | solution.py:15
  74.7 0.8 copy.119
  75.6 0.8 copy.128
  76.8 1.0 %copy.129 = bf16[1,128,2048]{2,1,0:T(8,128)(2,1)} copy(bf16[1,128,2048]{1,2,0:T(8,128)(2,1)S(1)} %bitcast.266) | data formatting | bytes 1048576
  77.8 9.9 %collective-permute-done.3 = bf16[2,1,128,512]{3,2,1,0:T(8,128)(2,1)} collective-permute-done((bf16[2,1,128,512]{3,2,1,0:T(8,128)(2,1)}, bf16[2,1,128,512]{3,2,1,0:T(8,128)(2,1)}, u32[]{:S(2)}, u32[]{:S(2)}) %collective-permute-start.3) | collective-permute-done | bytes 262176 | tf_op jit(solution)/shard_map/ppermute | solution.py:15
  87.7 1.9 %fusion.41 = (bf16[1,128,512]{2,1,0:T(8,128)(2,1)}, bf16[1,128,512]{2,1,0:T(8,128)(2,1)}) fusion(f32[1,128,512]{2,1,0:T(8,128)S(1)} %copy-done.4, bf16[2,1,128,512]{3,2,1,0:T(8,128)(2,1)} %collective-permute-done.3, bf16[2,1,128,512]{3,2,1,0:T(8,128)(2,1)} %collective-permute-done.2, f32[1,128,512]{2,1,0:T(8,128)S(1)} %copy-done.3), kind=kLoop, calls=%fused_computation.60 | loop fusion | flops 655360 | bytes 1310720 | tf_op jit(solution)/shard_map/convert_element_type | solution.py:99
  (63 shorter events, 5.3 us)
Async XLA Ops:
  0.6 10.7 %copy-start.13 = (f32[16,128,1]{1,2,0:T(1,128)S(1)}, f32[16,128,1]{1,2,0:T(1,128)}, u32[]{:S(2)}) copy-start(f32[16,128,1]{1,2,0:T(1,128)} %param.12) | copy-start | bytes 24580
  0.6 10.8 %copy-start.6 = (bf16[16,128,128]{2,1,0:T(8,128)(2,1)S(1)}, bf16[16,128,128]{2,1,0:T(8,128)(2,1)}, u32[]{:S(2)}) copy-start(bf16[16,128,128]{2,1,0:T(8,128)(2,1)} %param.10) | copy-start | bytes 1572868
  2.8 33.9 %collective-permute-start = (bf16[2,1,128,512]{2,3,1,0:T(8,128)(2,1)S(1)}, bf16[2,1,128,512]{2,3,1,0:T(8,128)(2,1)}, u32[]{:S(2)}, u32[]{:S(2)}) collective-permute-start(bf16[2,1,128,512]{2,3,1,0:T(8,128)(2,1)S(1)} %pad_maximum_fusion.1), channel_id=1, source_target_pairs={{0,16},{16,32},{32,48},{48,64},{64,80},{80,96},{96,112},{112,128},... | collective-permute-start | bytes 786440 | tf_op jit(solution)/shard_map/ppermute | solution.py:15
  4.7 33.6 %collective-permute-start.1 = (bf16[2,1,128,512]{2,3,1,0:T(8,128)(2,1)S(1)}, bf16[2,1,128,512]{2,3,1,0:T(8,128)(2,1)S(1)}, u32[]{:S(2)}, u32[]{:S(2)}) collective-permute-start(bf16[2,1,128,512]{2,3,1,0:T(8,128)(2,1)S(1)} %pad_maximum_fusion.1), channel_id=1, source_target_pairs={{0,32},{16,48},{32,64},{48,80},{64,96},{80,112},{96,128},{112,144}... | collective-permute-start | bytes 786440 | tf_op jit(solution)/shard_map/ppermute | solution.py:15
  11.4 23.2 %copy-start.14 = (s32[128]{0:T(128)S(1)}, s32[128]{0:T(128)}, u32[]{:S(2)}) copy-start(s32[128]{0:T(128)} %param.13) | copy-start | bytes 1540
  11.5 23.8 %copy-start.8 = (bf16[1,128,512]{2,1,0:T(8,128)(2,1)S(1)}, bf16[1,128,512]{2,1,0:T(8,128)(2,1)}, u32[]{:S(2)}) copy-start(bf16[1,128,512]{2,1,0:T(8,128)(2,1)} %param.8) | copy-start | bytes 393220
  11.5 23.8 %copy-start.9 = (bf16[1,128,512]{2,1,0:T(8,128)(2,1)S(1)}, bf16[1,128,512]{2,1,0:T(8,128)(2,1)}, u32[]{:S(2)}) copy-start(bf16[1,128,512]{2,1,0:T(8,128)(2,1)} %param.9) | copy-start | bytes 393220
  12.4 23.6 %copy-start.7 = (bf16[1,128,2048]{2,1,0:T(8,128)(2,1)S(1)}, bf16[1,128,2048]{2,1,0:T(8,128)(2,1)}, u32[]{:S(2)}) copy-start(bf16[1,128,2048]{2,1,0:T(8,128)(2,1)} %param.7) | copy-start | bytes 1572868
  12.4 42.3 %all-to-all-start = ((bf16[16,131,128]{2,1,0:T(8,128)(2,1)}), bf16[16,131,128]{2,1,0:T(8,128)(2,1)S(1)}, u32[]{:S(2)}, u32[]{:S(2)}) async-start(bf16[16,131,128]{2,1,0:T(8,128)(2,1)} %pad_maximum_fusion), calls=%async_computation | async-start | bytes 1114112 | tf_op jit(solution)/shard_map/all_to_all | solution.py:45
  34.6 1.7 %copy-start.1 = (bf16[1,128,2048]{2,1,0:T(8,128)(2,1)S(1)}, bf16[1,128,2048]{2,1,0:T(8,128)(2,1)}, u32[]{:S(2)}) copy-start(bf16[1,128,2048]{2,1,0:T(8,128)(2,1)} %param.11) | copy-start | bytes 1572868
  58.3 0.9 %copy-start.5 = (bf16[128,4,128]{2,1,0:T(4,128)(2,1)S(1)}, bf16[128,4,128]{2,1,0:T(4,128)(2,1)}, u32[]{:S(2)}) copy-start(bf16[128,4,128]{2,1,0:T(4,128)(2,1)} %reshape.487) | copy-start | bytes 393220
  59.8 0.9 %copy-start.2 = (bf16[1,1,128,512]{2,3,1,0:T(8,128)(2,1)S(1)}, bf16[1,1,128,512]{2,3,1,0:T(8,128)(2,1)}, u32[]{:S(2)}) copy-start(bf16[1,1,128,512]{2,3,1,0:T(8,128)(2,1)} %get-tuple-element.17) | copy-start | bytes 393220
  61.1 1.0 %copy-start.11 = (bf16[1,1,128,512]{2,3,1,0:T(8,128)(2,1)S(1)}, bf16[1,1,128,512]{2,3,1,0:T(8,128)(2,1)}, u32[]{:S(2)}) copy-start(bf16[1,1,128,512]{2,3,1,0:T(8,128)(2,1)} %get-tuple-element.16) | copy-start | bytes 393220
  64.4 1.0 %copy-start.10 = (bf16[1,1,128,512]{2,3,1,0:T(8,128)(2,1)S(1)}, bf16[1,1,128,512]{2,3,1,0:T(8,128)(2,1)}, u32[]{:S(2)}) copy-start(bf16[1,1,128,512]{2,3,1,0:T(8,128)(2,1)} %get-tuple-element.14) | copy-start | bytes 393220
  65.7 0.9 %copy-start.12 = (bf16[4,128,128]{1,2,0:T(8,128)(2,1)S(1)}, bf16[4,128,128]{1,2,0:T(8,128)(2,1)}, u32[]{:S(2)}) copy-start(bf16[4,128,128]{1,2,0:T(8,128)(2,1)} %fusion.32) | copy-start | bytes 393220
  67.5 10.3 %collective-permute-start.2 = (bf16[2,1,128,512]{3,2,1,0:T(8,128)(2,1)}, bf16[2,1,128,512]{3,2,1,0:T(8,128)(2,1)}, u32[]{:S(2)}, u32[]{:S(2)}) collective-permute-start(bf16[2,1,128,512]{3,2,1,0:T(8,128)(2,1)} %pad_maximum_fusion.2), channel_id=1, source_target_pairs={{0,1008},{16,0},{32,16},{48,32},{64,48},{80,64},{96,80},{112,96},{... | collective-permute-start | bytes 786440 | tf_op jit(solution)/shard_map/ppermute | solution.py:15
  69.4 7.0 %copy-start = (f32[4,128,4,128]{3,1,2,0:T(8,128)S(1)}, f32[4,128,4,128]{3,1,2,0:T(8,128)}, u32[]{:S(2)}) copy-start(f32[4,128,4,128]{3,1,2,0:T(8,128)} %fusion.47) | copy-start | bytes 3145732
  72.8 14.8 %collective-permute-start.3 = (bf16[2,1,128,512]{3,2,1,0:T(8,128)(2,1)}, bf16[2,1,128,512]{3,2,1,0:T(8,128)(2,1)}, u32[]{:S(2)}, u32[]{:S(2)}) collective-permute-start(bf16[2,1,128,512]{3,2,1,0:T(8,128)(2,1)} %pad_maximum_fusion.3), channel_id=1, source_target_pairs={{0,992},{16,1008},{32,0},{48,16},{64,32},{80,48},{96,64},{112,80},... | collective-permute-start | bytes 786440 | tf_op jit(solution)/shard_map/ppermute | solution.py:15
  76.7 10.9 %copy-start.3 = (f32[1,128,512]{2,1,0:T(8,128)S(1)}, f32[1,128,512]{2,1,0:T(8,128)}, u32[]{:S(2)}) copy-start(f32[1,128,512]{2,1,0:T(8,128)} %copy.119) | copy-start | bytes 786436
  76.7 10.9 %copy-start.4 = (f32[1,128,512]{2,1,0:T(8,128)S(1)}, f32[1,128,512]{2,1,0:T(8,128)}, u32[]{:S(2)}) copy-start(f32[1,128,512]{2,1,0:T(8,128)} %copy.128) | copy-start | bytes 786436

commit v3 on v1

--- a/solution.py
+++ b/solution.py
@@ -33,28 +33,26 @@
     kv_ahead = [passed_along(own_kv, "ctx", step) for step in range(1, CYCLE_STEPS)]
 
     outputs = lax.all_to_all(attn_out, "head", split_axis=0, concat_axis=2, tiled=True)
-    lse_rows = lax.all_to_all(logsumexp, "head", split_axis=0, concat_axis=2, tiled=True)
 
     q5 = query.reshape(seq_count, tok_rows, KV_HEADS, group, HEAD_DIM)
     g5 = grad_out.reshape(seq_count, tok_rows, KV_HEADS, group, HEAD_DIM)
     o5 = outputs.reshape(seq_count, tok_rows, KV_HEADS, group, HEAD_DIM)
     delta_rows = jnp.sum(o5.astype(jnp.float32) * g5.astype(jnp.float32), axis=4)
     delta_heads = jnp.transpose(delta_rows, (0, 2, 3, 1))
-    lse_heads = jnp.transpose(
-        lse_rows.reshape(seq_count, tok_rows, KV_HEADS, group), (0, 2, 3, 1)
-    )
     query_pos = shard_positions(here)
 
-    def block_grads(kv_blk, key_pos):
+    def scaled_scores(kv_blk, key_pos):
         keys_here = kv_blk[0].reshape(seq_count, tok_rows, KV_HEADS, HEAD_DIM)
-        values_here = kv_blk[1].reshape(seq_count, tok_rows, KV_HEADS, HEAD_DIM)
         scores = jnp.einsum(
             "sqgrd,skgd->sgrqk", q5, keys_here, preferred_element_type=jnp.float32
         )
         allowed = key_pos[None, :] <= query_pos[:, None]
-        attn_probs = jnp.exp(
-            jnp.where(allowed, scores * score_scale - lse_heads[..., None], -jnp.inf)
-        )
+        return jnp.where(allowed, scores * score_scale, -jnp.inf)
+
+    def block_grads(kv_blk, masked, lse_heads):
+        keys_here = kv_blk[0].reshape(seq_count, tok_rows, KV_HEADS, HEAD_DIM)
+        values_here = kv_blk[1].reshape(seq_count, tok_rows, KV_HEADS, HEAD_DIM)
+        attn_probs = jnp.exp(masked - lse_heads[..., None])
         dprobs = jnp.einsum(
             "sqgrd,skgd->sgrqk", g5, values_here, preferred_element_type=jnp.float32
         )
@@ -75,10 +73,20 @@
         flat = (seq_count, tok_rows, KV_HEADS * HEAD_DIM)
         return query_part, key_part.reshape(flat), value_part.reshape(flat)
 
-    query_sum, key_sum, value_sum = block_grads(own_kv, query_pos)
+    blocks = [own_kv] + kv_ahead
+    masked = [
+        scaled_scores(blocks[step], shard_positions((here - step) % cycle_size))
+        for step in range(CYCLE_STEPS)
+    ]
+    row_max = masked[0].max(axis=-1)
     for step in range(1, CYCLE_STEPS):
-        source = (here - step) % cycle_size
-        part_query, part_key, part_value = block_grads(kv_ahead[step - 1], shard_positions(source))
+        row_max = jnp.maximum(row_max, masked[step].max(axis=-1))
+    row_sum = sum(jnp.exp(m - row_max[..., None]).sum(axis=-1) for m in masked)
+    lse_heads = row_max + jnp.log(row_sum)
+
+    query_sum, key_sum, value_sum = block_grads(own_kv, masked[0], lse_heads)
+    for step in range(1, CYCLE_STEPS):
+        part_query, part_key, part_value = block_grads(blocks[step], masked[step], lse_heads)
         query_sum = query_sum + part_query
         returned = passed_along(
             jnp.stack((part_key, part_value)).astype(jnp.bfloat16), "ctx", -step

time: 96 us -> 80.6 us (0.84)
  waiting for transfers between devices: 22.7 us -> 12.7 us
  starting transfers between devices: 43.9 us -> 34.6 us
  matrix products: 8.15 us -> 10.1 us
  local copies, waits for them, and re-layouts: 12.3 us -> 14 us
    all_to_all x1 -> x0, starting transfers between devices: 22.1 us -> none  [shards(): lax.all_to_all(logsumexp, 'head', split_axis=0, concat_axis=2, tiled=True)]
    all_to_all x1, starting transfers between devices: 9.31 us -> 22.2 us  [shards(): lax.all_to_all(attn_out, 'head', split_axis=0, concat_axis=2, tiled=True)]
    all_to_all x1, waiting for transfers between devices: 7.52 us -> 1.28 us  [shards(): lax.all_to_all(attn_out, 'head', split_axis=0, concat_axis=2, tiled=True)]
    all_to_all x1 -> x0, waiting for transfers between devices: 3.72 us -> none  [shards(): lax.all_to_all(logsumexp, 'head', split_axis=0, concat_axis=2, tiled=True)]
    dot_general x3, matrix products: 1.54 us -> 4.2 us  [block_grads(): jnp.einsum('sgrqk,sqgrd->skgd', attn_probs.astype(jnp.bfloat16), g5, pref...]
    unnamed x37 -> x33, local copies, waits for them, and re-layouts: 4 us -> 3.84 us
  transfers between devices with their start and end apart: 6 -> 5, of which waited for: 4 -> 3; matrix products, arithmetic and copies ran while one was open for 14% -> 22% of each run, Pallas kernels for 0% -> 0%
where the time goes in v3:
time: 80.6 us; the launch traced here: 80 us
  starting transfers between devices  34.6 us (43%)
  local copies, waits for them, and re-layouts  14 us (17%)
  waiting for transfers between devices  12.7 us (16%)
  matrix products  10.1 us (13%)
  other arithmetic  7.61 us (9%)
  between operations  1.03 us (1%)
    all_to_all x1, starting transfers between devices, shards(): lax.all_to_all(attn_out, 'head', split_axis=0, concat_axis=2, tiled=True)  22.2 us
    ppermute x4, starting transfers between devices, passed_along(): return lax.ppermute(value, axis, pairs)  12.4 us
    ppermute x4, waiting for transfers between devices, passed_along(): return lax.ppermute(value, axis, pairs)  11.4 us
    dot_general x3, matrix products, block_grads(): jnp.einsum('sgrqk,sqgrd->skgd', attn_probs.astype(jnp.bfloat16), g5, pref...  4.2 us
    another operation x4, local copies, waits for them, and re-layouts, shards(): jnp.stack((part_key, part_value)).astype(jnp.bfloat16)  4.19 us
    unnamed x33, local copies, waits for them, and re-layouts  3.84 us
    dot_general x3, matrix products, block_grads(): jnp.einsum('sgrqk,skgd->sqgrd', dscores, keys_here, preferred_element_typ...  2.84 us
    another operation x2, other arithmetic, shards(): jnp.stack((part_key, part_value)).astype(jnp.bfloat16)  2.39 us
  transfers between devices with their start and end apart: 5, of which 3 were waited for; matrix products, arithmetic and copies ran while one was open for 22% of the time, Pallas kernels for 0%

profile of v3, /device:TPU:118, one launch (start us, length us, event | category | flops | bytes accessed | tf_op | source)
XLA Modules:
  0.0 80.0 jit_solution(12466233149949904866)
XLA Ops:
  0.6 1.1 %copy.45 = bf16[1,128,512]{1,2,0:T(8,128)(2,1)S(1)} copy(bf16[1,128,512]{2,1,0:T(8,128)(2,1)} %param.8) | data formatting | bytes 262144 | tf_op args[1]
  1.8 0.7 pad_maximum_fusion
  2.6 1.9 %collective-permute-start = (bf16[2,1,128,512]{2,3,1,0:T(8,128)(2,1)}, bf16[2,1,128,512]{2,3,1,0:T(8,128)(2,1)S(1)}, u32[]{:S(2)}, u32[]{:S(2)}) collective-permute-start(bf16[2,1,128,512]{2,3,1,0:T(8,128)(2,1)} %pad_maximum_fusion), channel_id=1, source_target_pairs={{0,16},{16,32},{32,48},{48,64},{64,80},{80,96},{96,112},{112,128},... | collective-permute-start | bytes 786440 | tf_op jit(solution)/shard_map/ppermute | solution.py:15
  4.5 6.6 %collective-permute-start.1 = (bf16[2,1,128,512]{2,3,1,0:T(8,128)(2,1)}, bf16[2,1,128,512]{2,3,1,0:T(8,128)(2,1)}, u32[]{:S(2)}, u32[]{:S(2)}) collective-permute-start(bf16[2,1,128,512]{2,3,1,0:T(8,128)(2,1)} %pad_maximum_fusion), channel_id=1, source_target_pairs={{0,32},{16,48},{32,64},{48,80},{64,96},{80,112},{96,128},{112,144}... | collective-permute-start | bytes 786440 | tf_op jit(solution)/shard_map/ppermute | solution.py:15
  11.1 22.2 %all-to-all-start = ((bf16[16,128,128]{2,1,0:T(8,128)(2,1)}), bf16[16,128,128]{2,1,0:T(8,128)(2,1)}, u32[]{:S(2)}, u32[]{:S(2)}) async-start(bf16[16,128,128]{2,1,0:T(8,128)(2,1)} %param.10), calls=%async_computation | async-start | bytes 1048576 | tf_op jit(solution)/shard_map/all_to_all | solution.py:35
  33.5 0.7 reshape.456
  34.1 0.7 copy-done.14
  35.8 0.6 copy-done.4
  36.8 0.4 fusion.48
  37.2 0.7 fusion.45
  38.2 1.6 %fusion.46 = (bf16[1,1,128,512]{2,3,1,0:T(8,128)(2,1)}, bf16[1,1,128,512]{2,3,1,0:T(8,128)(2,1)S(1)}) fusion(bf16[2,1,128,512]{2,3,1,0:T(8,128)(2,1)} %collective-permute-done.1), kind=kLoop, calls=%fused_computation.89 | loop fusion | bytes 524288 | tf_op jit(solution)/shard_map/slice | solution.py:54
  40.3 0.7 exponential_reduce_fusion.1
  41.3 1.0 %fusion.26 = bf16[4,128,128]{1,2,0:T(8,128)(2,1)} fusion(bf16[128,4,4,128]{0,3,2,1:T(8,128)(2,1)S(1)} %bitcast.263, f32[1,4,4,128,128]{3,4,2,1,0:T(8,128)S(1)} %get-tuple-element.30, f32[4,4,128]{2,1,0:T(4,128)S(1)} %bitcast.286), kind=kOutput, calls=%fused_computation.39 | convolution fusion | flops 67698688 | bytes 1712128 | tf_op jit(solution)/shard_map/sgrqk,sqgrd->skgd/dot_general | solution.py:67
  42.2 1.6 %copy.69 = bf16[1,1,128,512]{3,2,1,0:T(8,128)(2,1)} copy(bf16[1,1,128,512]{2,3,1,0:T(8,128)(2,1)} %bitcast.284) | data formatting | bytes 262144 | tf_op jit(solution)/shard_map/stack | solution.py:92
  43.9 2.2 %fusion.27 = bf16[4,128,128]{1,2,0:T(8,128)(2,1)} fusion(bf16[128,4,4,128]{0,3,2,1:T(8,128)(2,1)S(1)} %bitcast.264, f32[1,4,4,128,128]{3,4,2,1,0:T(8,128)} %copy-done, f32[4,4,128]{2,1,0:T(4,128)S(1)} %bitcast.287), kind=kOutput, calls=%fused_computation.40 | convolution fusion | flops 67698688 | bytes 1712128 | tf_op jit(solution)/shard_map/sgrqk,sqgrd->skgd/dot_general | solution.py:67
  46.1 1.7 %copy.76 = bf16[1,1,128,512]{3,2,1,0:T(8,128)(2,1)} copy(bf16[1,1,128,512]{2,3,1,0:T(8,128)(2,1)} %bitcast.285) | data formatting | bytes 262144 | tf_op jit(solution)/shard_map/stack | solution.py:92
  47.8 1.0 %fusion.37 = f32[4,128,128,1]{1,2,3,0:T(8,128)} fusion(bf16[128,4,4,128]{0,3,2,1:T(8,128)(2,1)S(1)} %bitcast.265, f32[1,4,4,128,128]{3,4,2,1,0:T(8,128)S(1)} %get-tuple-element.28, f32[4,4,128]{2,1,0:T(4,128)S(1)} %bitcast.288), kind=kOutput, calls=%fused_computation.57 | convolution fusion | flops 67633152 | bytes 1843200 | tf_op jit(solution)/shard_map/sgrqk,sqgrd->skgd/dot_general | solution.py:67
  48.8 1.8 %copy.79 = f32[1,128,512]{2,1,0:T(8,128)} copy(f32[1,128,512]{1,2,0:T(8,128)} %bitcast.275) | data formatting | bytes 524288 | tf_op jit(solution)/shard_map/reshape | solution.py:74
  50.5 1.3 %all-to-all-done = bf16[16,128,128]{2,1,0:T(8,128)(2,1)} async-done(((bf16[16,128,128]{2,1,0:T(8,128)(2,1)}), bf16[16,128,128]{2,1,0:T(8,128)(2,1)}, u32[]{:S(2)}, u32[]{:S(2)}) %all-to-all-start) | async-done | bytes 524320 | tf_op jit(solution)/shard_map/all_to_all | solution.py:35
  51.8 1.6 %fusion.28 = f32[128,16]{0,1:T(8,128)S(1)} fusion(bf16[16,128,128]{2,1,0:T(8,128)(2,1)} %all-to-all-done, bf16[1,128,2048]{2,1,0:T(8,128)(2,1)} %param.11), kind=kLoop, calls=%fused_computation.42 | loop fusion | flops 1046528 | bytes 1056768 | tf_op jit(solution)/shard_map/reduce_sum | solution.py:40
  54.1 1.3 %convolution_bitcast_fusion = f32[4,128,4,128]{3,1,2,0:T(8,128)} fusion(bf16[128,4,128,1]{0,2,3,1:T(8,128)(2,1)S(1)} %copy.86, bf16[4,4,128,128]{2,3,1,0:T(8,128)(2,1)S(1)} %fusion.18), kind=kOutput, calls=%fused_computation | convolution fusion | flops 67108864 | bytes 1703936 | tf_op jit(solution)/shard_map/sgrqk,skgd->sqgrd/dot_general | solution.py:60
  55.3 0.4 fusion.20
  56.0 1.3 %fusion.50 = f32[4,128,4,128]{3,1,2,0:T(8,128)} fusion(bf16[128,4,128,1]{0,2,3,1:T(8,128)(2,1)S(1)} %bitcast.273, bf16[4,4,128,128]{2,3,1,0:T(8,128)(2,1)S(1)} %fusion.20), kind=kOutput, calls=%fused_computation.93 | convolution fusion | flops 67108864 | bytes 1703936 | tf_op jit(solution)/shard_map/sgrqk,skgd->sqgrd/dot_general | solution.py:60
  57.3 0.4 fusion.19
  58.1 0.8 copy.68
  58.8 1.6 %pad_maximum_fusion.1 = bf16[2,1,128,512]{3,2,1,0:T(8,128)(2,1)} fusion(bf16[1,1,128,512]{3,2,1,0:T(8,128)(2,1)S(1)} %copy-done.13, bf16[1,1,128,512]{3,2,1,0:T(8,128)(2,1)} %copy.68), kind=kLoop, calls=%fused_computation.62 | loop fusion | flops 131072 | bytes 524288 | tf_op jit(solution)/shard_map/stack | solution.py:92
  60.5 1.9 %collective-permute-start.2 = (bf16[2,1,128,512]{3,2,1,0:T(8,128)(2,1)}, bf16[2,1,128,512]{3,2,1,0:T(8,128)(2,1)}, u32[]{:S(2)}, u32[]{:S(2)}) collective-permute-start(bf16[2,1,128,512]{3,2,1,0:T(8,128)(2,1)} %pad_maximum_fusion.1), channel_id=1, source_target_pairs={{0,1008},{16,0},{32,16},{48,32},{64,48},{80,64},{96,80},{112,96},{... | collective-permute-start | bytes 786440 | tf_op jit(solution)/shard_map/ppermute | solution.py:15
  62.5 0.7 pad_maximum_fusion.2
  63.3 1.9 %collective-permute-start.3 = (bf16[2,1,128,512]{3,2,1,0:T(8,128)(2,1)}, bf16[2,1,128,512]{3,2,1,0:T(8,128)(2,1)}, u32[]{:S(2)}, u32[]{:S(2)}) collective-permute-start(bf16[2,1,128,512]{3,2,1,0:T(8,128)(2,1)} %pad_maximum_fusion.2), channel_id=1, source_target_pairs={{0,992},{16,1008},{32,0},{48,16},{64,32},{80,48},{96,64},{112,80},... | collective-permute-start | bytes 786440 | tf_op jit(solution)/shard_map/ppermute | solution.py:15
  65.7 1.0 %copy.80 = bf16[1,128,2048]{2,1,0:T(8,128)(2,1)} copy(bf16[1,128,2048]{1,2,0:T(8,128)(2,1)S(1)} %bitcast.269) | data formatting | bytes 1048576
  66.8 11.3 %collective-permute-done.3 = bf16[2,1,128,512]{3,2,1,0:T(8,128)(2,1)} collective-permute-done((bf16[2,1,128,512]{3,2,1,0:T(8,128)(2,1)}, bf16[2,1,128,512]{3,2,1,0:T(8,128)(2,1)}, u32[]{:S(2)}, u32[]{:S(2)}) %collective-permute-start.3) | collective-permute-done | bytes 262176 | tf_op jit(solution)/shard_map/ppermute | solution.py:15
  78.1 1.9 %fusion.42 = (bf16[1,128,512]{2,1,0:T(8,128)(2,1)}, bf16[1,128,512]{2,1,0:T(8,128)(2,1)}) fusion(f32[1,128,512]{2,1,0:T(8,128)S(1)} %copy-done.5, bf16[2,1,128,512]{3,2,1,0:T(8,128)(2,1)} %collective-permute-done.3, bf16[2,1,128,512]{3,2,1,0:T(8,128)(2,1)} %collective-permute-done.2, f32[1,128,512]{2,1,0:T(8,128)S(1)} %copy.70), kind=kLoop, calls=%fused_computation.65 | loop fusion | flops 655360 | bytes 1310720 | tf_op jit(solution)/shard_map/convert_element_type | solution.py:97
  (55 shorter events, 4.5 us)
Async XLA Ops:
  0.6 1.1 %copy-start.9 = (bf16[1,128,512]{2,1,0:T(8,128)(2,1)S(1)}, bf16[1,128,512]{2,1,0:T(8,128)(2,1)}, u32[]{:S(2)}) copy-start(bf16[1,128,512]{2,1,0:T(8,128)(2,1)} %param.9) | copy-start | bytes 393220
  2.6 34.6 %collective-permute-start = (bf16[2,1,128,512]{2,3,1,0:T(8,128)(2,1)}, bf16[2,1,128,512]{2,3,1,0:T(8,128)(2,1)S(1)}, u32[]{:S(2)}, u32[]{:S(2)}) collective-permute-start(bf16[2,1,128,512]{2,3,1,0:T(8,128)(2,1)} %pad_maximum_fusion), channel_id=1, source_target_pairs={{0,16},{16,32},{32,48},{48,64},{64,80},{80,96},{96,112},{112,128},... | collective-permute-start | bytes 786440 | tf_op jit(solution)/shard_map/ppermute | solution.py:15
  4.5 33.7 %collective-permute-start.1 = (bf16[2,1,128,512]{2,3,1,0:T(8,128)(2,1)}, bf16[2,1,128,512]{2,3,1,0:T(8,128)(2,1)}, u32[]{:S(2)}, u32[]{:S(2)}) collective-permute-start(bf16[2,1,128,512]{2,3,1,0:T(8,128)(2,1)} %pad_maximum_fusion), channel_id=1, source_target_pairs={{0,32},{16,48},{32,64},{48,80},{64,96},{80,112},{96,128},{112,144}... | collective-permute-start | bytes 786440 | tf_op jit(solution)/shard_map/ppermute | solution.py:15
  11.1 22.3 %copy-start.8 = (bf16[1,128,512]{2,1,0:T(8,128)(2,1)S(1)}, bf16[1,128,512]{2,1,0:T(8,128)(2,1)}, u32[]{:S(2)}) copy-start(bf16[1,128,512]{2,1,0:T(8,128)(2,1)} %param.8) | copy-start | bytes 393220
  11.1 40.7 %all-to-all-start = ((bf16[16,128,128]{2,1,0:T(8,128)(2,1)}), bf16[16,128,128]{2,1,0:T(8,128)(2,1)}, u32[]{:S(2)}, u32[]{:S(2)}) async-start(bf16[16,128,128]{2,1,0:T(8,128)(2,1)} %param.10), calls=%async_computation | async-start | bytes 1048576 | tf_op jit(solution)/shard_map/all_to_all | solution.py:35
  33.3 2.0 %copy-start.7 = (bf16[1,128,2048]{2,1,0:T(8,128)(2,1)S(1)}, bf16[1,128,2048]{2,1,0:T(8,128)(2,1)}, u32[]{:S(2)}) copy-start(bf16[1,128,2048]{2,1,0:T(8,128)(2,1)} %param.7) | copy-start | bytes 1572868
  34.1 0.7 copy-start.14
  35.4 1.0 %copy-start.4 = (bf16[1,128,2048]{2,1,0:T(8,128)(2,1)S(1)}, bf16[1,128,2048]{2,1,0:T(8,128)(2,1)}, u32[]{:S(2)}) copy-start(bf16[1,128,2048]{2,1,0:T(8,128)(2,1)} %param.11) | copy-start | bytes 1572868
  40.2 1.0 %copy-start = (f32[1,4,4,128,128]{3,4,2,1,0:T(8,128)}, f32[1,4,4,128,128]{3,4,2,1,0:T(8,128)S(1)}, u32[]{:S(2)}) copy-start(f32[1,4,4,128,128]{3,4,2,1,0:T(8,128)S(1)} %get-tuple-element.26) | copy-start | bytes 3145732
  51.8 1.6 %copy-start.6 = (bf16[128,4,128]{2,1,0:T(4,128)(2,1)S(1)}, bf16[128,4,128]{2,1,0:T(4,128)(2,1)}, u32[]{:S(2)}) copy-start(bf16[128,4,128]{2,1,0:T(4,128)(2,1)} %reshape.456) | copy-start | bytes 393220
  54.1 1.3 %copy-start.1 = (f32[1,4,4,128,128]{3,4,2,1,0:T(8,128)S(1)}, f32[1,4,4,128,128]{3,4,2,1,0:T(8,128)}, u32[]{:S(2)}) copy-start(f32[1,4,4,128,128]{3,4,2,1,0:T(8,128)} %copy-done) | copy-start | bytes 3145732
  54.1 1.3 %copy-start.11 = (bf16[1,1,128,512]{2,3,1,0:T(8,128)(2,1)S(1)}, bf16[1,1,128,512]{2,3,1,0:T(8,128)(2,1)}, u32[]{:S(2)}) copy-start(bf16[1,1,128,512]{2,3,1,0:T(8,128)(2,1)} %get-tuple-element.16) | copy-start | bytes 393220
  56.0 1.3 %copy-start.10 = (bf16[1,1,128,512]{2,3,1,0:T(8,128)(2,1)S(1)}, bf16[1,1,128,512]{2,3,1,0:T(8,128)(2,1)}, u32[]{:S(2)}) copy-start(bf16[1,1,128,512]{2,3,1,0:T(8,128)(2,1)} %get-tuple-element.14) | copy-start | bytes 393220
  57.7 1.1 %copy-start.13 = (bf16[1,1,128,512]{3,2,1,0:T(8,128)(2,1)S(1)}, bf16[1,1,128,512]{3,2,1,0:T(8,128)(2,1)}, u32[]{:S(2)}) copy-start(bf16[1,1,128,512]{3,2,1,0:T(8,128)(2,1)} %copy.69) | copy-start | bytes 393220
  57.7 4.8 %copy-start.12 = (bf16[1,1,128,512]{3,2,1,0:T(8,128)(2,1)S(1)}, bf16[1,1,128,512]{3,2,1,0:T(8,128)(2,1)}, u32[]{:S(2)}) copy-start(bf16[1,1,128,512]{3,2,1,0:T(8,128)(2,1)} %copy.76) | copy-start | bytes 393220
  58.0 7.3 %copy-start.2 = (f32[4,128,4,128]{3,1,2,0:T(8,128)S(1)}, f32[4,128,4,128]{3,1,2,0:T(8,128)}, u32[]{:S(2)}) copy-start(f32[4,128,4,128]{3,1,2,0:T(8,128)} %convolution_bitcast_fusion) | copy-start | bytes 3145732
  58.1 7.3 %copy-start.3 = (f32[4,128,4,128]{3,1,2,0:T(8,128)S(1)}, f32[4,128,4,128]{3,1,2,0:T(8,128)}, u32[]{:S(2)}) copy-start(f32[4,128,4,128]{3,1,2,0:T(8,128)} %fusion.50) | copy-start | bytes 3145732
  60.5 6.3 %collective-permute-start.2 = (bf16[2,1,128,512]{3,2,1,0:T(8,128)(2,1)}, bf16[2,1,128,512]{3,2,1,0:T(8,128)(2,1)}, u32[]{:S(2)}, u32[]{:S(2)}) collective-permute-start(bf16[2,1,128,512]{3,2,1,0:T(8,128)(2,1)} %pad_maximum_fusion.1), channel_id=1, source_target_pairs={{0,1008},{16,0},{32,16},{48,32},{64,48},{80,64},{96,80},{112,96},{... | collective-permute-start | bytes 786440 | tf_op jit(solution)/shard_map/ppermute | solution.py:15
  63.3 14.8 %collective-permute-start.3 = (bf16[2,1,128,512]{3,2,1,0:T(8,128)(2,1)}, bf16[2,1,128,512]{3,2,1,0:T(8,128)(2,1)}, u32[]{:S(2)}, u32[]{:S(2)}) collective-permute-start(bf16[2,1,128,512]{3,2,1,0:T(8,128)(2,1)} %pad_maximum_fusion.2), channel_id=1, source_target_pairs={{0,992},{16,1008},{32,0},{48,16},{64,32},{80,48},{96,64},{112,80},... | collective-permute-start | bytes 786440 | tf_op jit(solution)/shard_map/ppermute | solution.py:15
  65.7 12.4 %copy-start.5 = (f32[1,128,512]{2,1,0:T(8,128)S(1)}, f32[1,128,512]{2,1,0:T(8,128)}, u32[]{:S(2)}) copy-start(f32[1,128,512]{2,1,0:T(8,128)} %copy.79) | copy-start | bytes 786436

commit v4 on v3

--- a/solution.py
+++ b/solution.py
@@ -61,17 +61,16 @@
             "sgrqk,skgd->sqgrd", dscores, keys_here, preferred_element_type=jnp.float32
         )
         key_part = (
-            jnp.einsum("sgrqk,sqgrd->skgd", dscores, q5, preferred_element_type=jnp.float32)
+            jnp.einsum("sgrqk,sqgrd->sgdk", dscores, q5, preferred_element_type=jnp.float32)
             * score_scale
         )
         value_part = jnp.einsum(
-            "sgrqk,sqgrd->skgd",
+            "sgrqk,sqgrd->sgdk",
             attn_probs.astype(jnp.bfloat16),
             g5,
             preferred_element_type=jnp.float32,
         )
-        flat = (seq_count, tok_rows, KV_HEADS * HEAD_DIM)
-        return query_part, key_part.reshape(flat), value_part.reshape(flat)
+        return query_part, key_part, value_part
 
     blocks = [own_kv] + kv_ahead
     masked = [
@@ -94,7 +93,10 @@
         key_sum = key_sum + returned[0].astype(jnp.float32)
         value_sum = value_sum + returned[1].astype(jnp.float32)
     query_grad = (query_sum * score_scale).astype(jnp.bfloat16).reshape(query.shape)
-    return (query_grad, key_sum.astype(jnp.bfloat16), value_sum.astype(jnp.bfloat16))
+    flat = (seq_count, tok_rows, KV_HEADS * HEAD_DIM)
+    key_grad = jnp.transpose(key_sum.astype(jnp.bfloat16), (0, 3, 1, 2)).reshape(flat)
+    value_grad = jnp.transpose(value_sum.astype(jnp.bfloat16), (0, 3, 1, 2)).reshape(flat)
+    return (query_grad, key_grad, value_grad)
 
 
 def solution(mesh):

time: 80.6 us -> 80.4 us (level)
  waiting for transfers between devices: 12.7 us -> 19.9 us
  local copies, waits for them, and re-layouts: 14 us -> 10.2 us
  other arithmetic: 7.61 us -> 4.84 us
  matrix products: 10.1 us -> 9.19 us
    all_to_all x1, waiting for transfers between devices: 1.28 us -> 8.9 us  [shards(): lax.all_to_all(attn_out, 'head', split_axis=0, concat_axis=2, tiled=True)]
    another operation x7 -> x3, local copies, waits for them, and re-layouts: 5.41 us -> 1.33 us  [the longest x4 4.19 us: shards(): jnp.stack((part_key, part_value)).astype(jnp.bfloat16)]
    unnamed x33 -> x27, local copies, waits for them, and re-layouts: 3.84 us -> 6.1 us
    dot_general x3, matrix products: 2.84 us -> 0.86 us  [block_grads(): jnp.einsum('sgrqk,skgd->sqgrd', dscores, keys_here, preferred_element_typ...]
    reshape x4 -> x2, local copies, waits for them, and re-layouts: 2.09 us -> 0.17 us  [the longest x2 1.91 us: block_grads(): return (query_part, key_part.reshape(flat), value_part.reshape(flat))]
    convert_element_type x1 -> x0, other arithmetic: 1.9 us -> none  [shards(): value_sum.astype(jnp.bfloat16)]
    another operation x2, other arithmetic: 2.39 us -> 1.45 us  [shards(): jnp.stack((part_key, part_value)).astype(jnp.bfloat16)]
    dot_general x3, matrix products: 1.05 us -> 1.96 us  [block_grads(): jnp.einsum('sqgrd,skgd->sgrqk', g5, values_here, preferred_element_type=j...]
  transfers between devices with their start and end apart: 5 -> 5, of which waited for: 3 -> 2; matrix products, arithmetic and copies ran while one was open for 22% -> 14% of each run, Pallas kernels for 0% -> 0%
where the time goes in v4:
time: 80.4 us; the launch traced here: 79.8 us
  starting transfers between devices  34.7 us (43%)
  waiting for transfers between devices  19.9 us (25%)
  local copies, waits for them, and re-layouts  10.2 us (13%)
  matrix products  9.19 us (11%)
  other arithmetic  4.84 us (6%)
  between operations  0.98 us (1%)
    all_to_all x1, starting transfers between devices, shards(): lax.all_to_all(attn_out, 'head', split_axis=0, concat_axis=2, tiled=True)  22.2 us
    ppermute x4, starting transfers between devices, passed_along(): return lax.ppermute(value, axis, pairs)  12.5 us
    ppermute x4, waiting for transfers between devices, passed_along(): return lax.ppermute(value, axis, pairs)  11 us
    all_to_all x1, waiting for transfers between devices, shards(): lax.all_to_all(attn_out, 'head', split_axis=0, concat_axis=2, tiled=True)  8.9 us
    unnamed x27, local copies, waits for them, and re-layouts  6.1 us
    dot_general x3, matrix products, block_grads(): jnp.einsum('sgrqk,sqgrd->sgdk', attn_probs.astype(jnp.bfloat16), g5, pref...  3.24 us
    slice x2, local copies, waits for them, and re-layouts, block_grads(): values_here = kv_blk[1].reshape(seq_count, tok_rows, KV_HEADS, HEAD_DIM)  2.32 us
    dot_general x3, matrix products, block_grads(): jnp.einsum('sgrqk,sqgrd->sgdk', dscores, q5, preferred_element_type=jnp.f...  2.02 us
  transfers between devices with their start and end apart: 5, of which 2 were waited for; matrix products, arithmetic and copies ran while one was open for 14% of the time, Pallas kernels for 0%

profile of v4, /device:TPU:118, one launch (start us, length us, event | category | flops | bytes accessed | tf_op | source)
XLA Modules:
  0.0 79.8 jit_solution(6890578489372019071)
XLA Ops:
  0.6 1.1 %copy.41 = bf16[1,128,512]{1,2,0:T(8,128)(2,1)S(1)} copy(bf16[1,128,512]{2,1,0:T(8,128)(2,1)} %param.8) | data formatting | bytes 262144 | tf_op args[1]
  1.8 0.7 pad_maximum_fusion
  2.6 1.9 %collective-permute-start = (bf16[2,1,128,512]{2,3,1,0:T(8,128)(2,1)}, bf16[2,1,128,512]{2,3,1,0:T(8,128)(2,1)S(1)}, u32[]{:S(2)}, u32[]{:S(2)}) collective-permute-start(bf16[2,1,128,512]{2,3,1,0:T(8,128)(2,1)} %pad_maximum_fusion), channel_id=1, source_target_pairs={{0,16},{16,32},{32,48},{48,64},{64,80},{80,96},{96,112},{112,128},... | collective-permute-start | bytes 786440 | tf_op jit(solution)/shard_map/ppermute | solution.py:15
  4.5 6.6 %collective-permute-start.1 = (bf16[2,1,128,512]{2,3,1,0:T(8,128)(2,1)}, bf16[2,1,128,512]{2,3,1,0:T(8,128)(2,1)}, u32[]{:S(2)}, u32[]{:S(2)}) collective-permute-start(bf16[2,1,128,512]{2,3,1,0:T(8,128)(2,1)} %pad_maximum_fusion), channel_id=1, source_target_pairs={{0,32},{16,48},{32,64},{48,80},{64,96},{80,112},{96,128},{112,144}... | collective-permute-start | bytes 786440 | tf_op jit(solution)/shard_map/ppermute | solution.py:15
  11.1 22.2 %all-to-all-start = ((bf16[16,128,128]{2,1,0:T(8,128)(2,1)}), bf16[16,128,128]{2,1,0:T(8,128)(2,1)}, u32[]{:S(2)}, u32[]{:S(2)}) async-start(bf16[16,128,128]{2,1,0:T(8,128)(2,1)} %param.10), calls=%async_computation | async-start | bytes 1048576 | tf_op jit(solution)/shard_map/all_to_all | solution.py:35
  33.5 0.7 reshape.379
  34.2 0.7 copy-done.10
  35.9 0.5 copy-done.2
  36.8 0.4 fusion.60
  37.2 0.7 fusion.57
  37.9 0.4 fusion.61
  38.3 1.6 %fusion.58 = (bf16[1,1,128,512]{2,3,1,0:T(8,128)(2,1)}, bf16[1,1,128,512]{2,3,1,0:T(8,128)(2,1)S(1)}) fusion(bf16[2,1,128,512]{2,3,1,0:T(8,128)(2,1)} %collective-permute-done.1), kind=kLoop, calls=%fused_computation.100 | loop fusion | bytes 524288 | tf_op jit(solution)/shard_map/slice | solution.py:54
  39.9 0.4 fusion.59
  40.3 0.7 exponential_reduce_fusion.1
  41.0 1.0 %fusion.30 = bf16[1,1,4,128,128]{4,3,2,1,0:T(8,128)(2,1)} fusion(bf16[128,4,4,128]{0,3,2,1:T(8,128)(2,1)S(1)} %bitcast.250, f32[1,4,4,128,128]{3,4,2,1,0:T(8,128)S(1)} %get-tuple-element.28, f32[4,4,128]{2,1,0:T(4,128)S(1)} %bitcast.268), kind=kOutput, calls=%fused_computation.44 | convolution fusion | flops 67698688 | bytes 1712128 | tf_op jit(solution)/shard_map/sgrqk,sqgrd->sgdk/dot_general | solution.py:67
  41.9 1.0 %fusion.29 = bf16[1,1,4,128,128]{4,3,2,1,0:T(8,128)(2,1)} fusion(bf16[128,4,4,128]{0,3,2,1:T(8,128)(2,1)S(1)} %bitcast.251, f32[1,4,4,128,128]{3,4,2,1,0:T(8,128)S(1)} %get-tuple-element.24, f32[4,4,128]{2,1,0:T(4,128)S(1)} %bitcast.269), kind=kOutput, calls=%fused_computation.43 | convolution fusion | flops 67698688 | bytes 1712128 | tf_op jit(solution)/shard_map/sgrqk,sqgrd->sgdk/dot_general | solution.py:67
  42.9 8.9 %all-to-all-done = bf16[16,128,128]{2,1,0:T(8,128)(2,1)} async-done(((bf16[16,128,128]{2,1,0:T(8,128)(2,1)}), bf16[16,128,128]{2,1,0:T(8,128)(2,1)}, u32[]{:S(2)}, u32[]{:S(2)}) %all-to-all-start) | async-done | bytes 524320 | tf_op jit(solution)/shard_map/all_to_all | solution.py:35
  51.8 1.6 %fusion.33 = f32[128,16]{0,1:T(8,128)S(1)} fusion(bf16[16,128,128]{2,1,0:T(8,128)(2,1)} %all-to-all-done, bf16[1,128,2048]{2,1,0:T(8,128)(2,1)} %param.11), kind=kLoop, calls=%fused_computation.48 | loop fusion | flops 1046528 | bytes 1056768 | tf_op jit(solution)/shard_map/reduce_sum | solution.py:40
  53.5 1.3 %fusion.20 = bf16[4,4,128,128]{2,3,1,0:T(8,128)(2,1)S(1)} fusion(bf16[128,4,128,1]{0,2,3,1:T(8,128)(2,1)} %bitcast.264, bf16[128,4,4,128]{0,3,2,1:T(8,128)(2,1)S(1)} %bitcast.252, f32[1,4,4,128,128]{3,4,2,1,0:T(8,128)S(1)} %copy-done.1, f32[4,4,128]{2,1,0:T(4,128)S(1)} %bitcast.274, f32[4,4,128]{2,1,0:T(4,128)S(1)} %bitcast.270), kind=kOutput, calls=%fused_computation.28 | convolution fusion | flops 68157440 | bytes 2244608 | tf_op jit(solution)/shard_map/sqgrd,skgd->sgrqk/dot_general | solution.py:56
  55.4 0.6 copy-done.7
  56.0 0.4 fusion.19
  56.8 0.5 copy-done.9
  57.3 0.7 pad_maximum_fusion.1
  58.0 2.0 %collective-permute-start.2 = (bf16[2,1,4,128,128]{4,3,2,1,0:T(8,128)(2,1)}, bf16[2,1,4,128,128]{4,3,2,1,0:T(8,128)(2,1)}, u32[]{:S(2)}, u32[]{:S(2)}) collective-permute-start(bf16[2,1,4,128,128]{4,3,2,1,0:T(8,128)(2,1)} %pad_maximum_fusion.1), channel_id=1, source_target_pairs={{0,1008},{16,0},{32,16},{48,32},{64,48},{80,64},{96,80},{112,96},{... | collective-permute-start | bytes 786440 | tf_op jit(solution)/shard_map/ppermute | solution.py:15
  60.1 0.7 pad_maximum_fusion.2
  60.8 1.9 %collective-permute-start.3 = (bf16[2,1,4,128,128]{4,3,2,1,0:T(8,128)(2,1)}, bf16[2,1,4,128,128]{4,3,2,1,0:T(8,128)(2,1)}, u32[]{:S(2)}, u32[]{:S(2)}) collective-permute-start(bf16[2,1,4,128,128]{4,3,2,1,0:T(8,128)(2,1)} %pad_maximum_fusion.2), channel_id=1, source_target_pairs={{0,992},{16,1008},{32,0},{48,16},{64,32},{80,48},{96,64},{112,80},... | collective-permute-start | bytes 786440 | tf_op jit(solution)/shard_map/ppermute | solution.py:15
  63.7 1.0 %copy.70 = bf16[1,128,2048]{2,1,0:T(8,128)(2,1)} copy(bf16[1,128,2048]{1,2,0:T(8,128)(2,1)S(1)} %bitcast.256) | data formatting | bytes 1048576
  64.7 11.0 %collective-permute-done.3 = bf16[2,1,4,128,128]{4,3,2,1,0:T(8,128)(2,1)} collective-permute-done((bf16[2,1,4,128,128]{4,3,2,1,0:T(8,128)(2,1)}, bf16[2,1,4,128,128]{4,3,2,1,0:T(8,128)(2,1)}, u32[]{:S(2)}, u32[]{:S(2)}) %collective-permute-start.3) | collective-permute-done | bytes 262176 | tf_op jit(solution)/shard_map/ppermute | solution.py:15
  75.6 1.3 %fusion.46 = bf16[4,128,128]{2,1,0:T(8,128)(2,1)S(1)} fusion(bf16[2,1,4,128,128]{4,3,2,1,0:T(8,128)(2,1)} %collective-permute-done.3, bf16[2,1,4,128,128]{4,3,2,1,0:T(8,128)(2,1)} %collective-permute-done.2, bf16[128,4,4,128]{0,3,2,1:T(8,128)(2,1)S(1)} %bitcast.255, f32[1,4,4,128,128]{3,4,2,1,0:T(8,128)S(1)} %get-tuple-element.26, ...), kind=kOutput, calls=%fused_computation.70 | convolution fusion | flops 67960832 | bytes 1974272 | tf_op jit(solution)/shard_map/sgrqk,sqgrd->sgdk/dot_general | solution.py:67
  76.9 0.8 copy.72
  77.7 1.3 %fusion.47 = bf16[4,128,128]{2,1,0:T(8,128)(2,1)S(1)} fusion(bf16[2,1,4,128,128]{4,3,2,1,0:T(8,128)(2,1)} %collective-permute-done.3, bf16[2,1,4,128,128]{4,3,2,1,0:T(8,128)(2,1)} %collective-permute-done.2, bf16[4,4,128,128]{2,3,1,0:T(8,128)(2,1)S(1)} %fusion.18, bf16[128,4,4,128]{3,2,1,0:T(4,128)(2,1)S(1)} %reshape.376), kind=kOutput, calls=%fused_computation.73 | convolution fusion | flops 67502080 | bytes 1441792 | tf_op jit(solution)/shard_map/sgrqk,sqgrd->sgdk/dot_general | solution.py:64
  79.0 0.8 copy.71
  (42 shorter events, 3.5 us)
Async XLA Ops:
  0.6 1.1 %copy-start.6 = (bf16[1,128,512]{2,1,0:T(8,128)(2,1)S(1)}, bf16[1,128,512]{2,1,0:T(8,128)(2,1)}, u32[]{:S(2)}) copy-start(bf16[1,128,512]{2,1,0:T(8,128)(2,1)} %param.9) | copy-start | bytes 393220
  2.6 34.6 %collective-permute-start = (bf16[2,1,128,512]{2,3,1,0:T(8,128)(2,1)}, bf16[2,1,128,512]{2,3,1,0:T(8,128)(2,1)S(1)}, u32[]{:S(2)}, u32[]{:S(2)}) collective-permute-start(bf16[2,1,128,512]{2,3,1,0:T(8,128)(2,1)} %pad_maximum_fusion), channel_id=1, source_target_pairs={{0,16},{16,32},{32,48},{48,64},{64,80},{80,96},{96,112},{112,128},... | collective-permute-start | bytes 786440 | tf_op jit(solution)/shard_map/ppermute | solution.py:15
  4.5 33.8 %collective-permute-start.1 = (bf16[2,1,128,512]{2,3,1,0:T(8,128)(2,1)}, bf16[2,1,128,512]{2,3,1,0:T(8,128)(2,1)}, u32[]{:S(2)}, u32[]{:S(2)}) collective-permute-start(bf16[2,1,128,512]{2,3,1,0:T(8,128)(2,1)} %pad_maximum_fusion), channel_id=1, source_target_pairs={{0,32},{16,48},{32,64},{48,80},{64,96},{80,112},{96,128},{112,144}... | collective-permute-start | bytes 786440 | tf_op jit(solution)/shard_map/ppermute | solution.py:15
  11.1 22.3 %copy-start.5 = (bf16[1,128,512]{2,1,0:T(8,128)(2,1)S(1)}, bf16[1,128,512]{2,1,0:T(8,128)(2,1)}, u32[]{:S(2)}) copy-start(bf16[1,128,512]{2,1,0:T(8,128)(2,1)} %param.8) | copy-start | bytes 393220
  11.1 40.7 %all-to-all-start = ((bf16[16,128,128]{2,1,0:T(8,128)(2,1)}), bf16[16,128,128]{2,1,0:T(8,128)(2,1)}, u32[]{:S(2)}, u32[]{:S(2)}) async-start(bf16[16,128,128]{2,1,0:T(8,128)(2,1)} %param.10), calls=%async_computation | async-start | bytes 1048576 | tf_op jit(solution)/shard_map/all_to_all | solution.py:35
  33.3 2.0 %copy-start.4 = (bf16[1,128,2048]{2,1,0:T(8,128)(2,1)S(1)}, bf16[1,128,2048]{2,1,0:T(8,128)(2,1)}, u32[]{:S(2)}) copy-start(bf16[1,128,2048]{2,1,0:T(8,128)(2,1)} %param.7) | copy-start | bytes 1572868
  34.2 0.7 copy-start.10
  35.4 1.0 %copy-start.2 = (bf16[1,128,2048]{2,1,0:T(8,128)(2,1)S(1)}, bf16[1,128,2048]{2,1,0:T(8,128)(2,1)}, u32[]{:S(2)}) copy-start(bf16[1,128,2048]{2,1,0:T(8,128)(2,1)} %param.11) | copy-start | bytes 1572868
  40.3 1.7 %copy-start = (f32[1,4,4,128,128]{3,4,2,1,0:T(8,128)}, f32[1,4,4,128,128]{3,4,2,1,0:T(8,128)S(1)}, u32[]{:S(2)}) copy-start(f32[1,4,4,128,128]{3,4,2,1,0:T(8,128)S(1)} %get-tuple-element.24) | copy-start | bytes 3145732
  51.8 1.6 %copy-start.1 = (f32[1,4,4,128,128]{3,4,2,1,0:T(8,128)S(1)}, f32[1,4,4,128,128]{3,4,2,1,0:T(8,128)}, u32[]{:S(2)}) copy-start(f32[1,4,4,128,128]{3,4,2,1,0:T(8,128)} %copy-done) | copy-start | bytes 3145732
  55.1 0.9 %copy-start.7 = (bf16[1,1,128,512]{2,3,1,0:T(8,128)(2,1)S(1)}, bf16[1,1,128,512]{2,3,1,0:T(8,128)(2,1)}, u32[]{:S(2)}) copy-start(bf16[1,1,128,512]{2,3,1,0:T(8,128)(2,1)} %get-tuple-element.12) | copy-start | bytes 393220
  56.4 0.9 %copy-start.9 = (bf16[1,1,4,128,128]{4,3,2,1,0:T(8,128)(2,1)S(1)}, bf16[1,1,4,128,128]{4,3,2,1,0:T(8,128)(2,1)}, u32[]{:S(2)}) copy-start(bf16[1,1,4,128,128]{4,3,2,1,0:T(8,128)(2,1)} %fusion.30) | copy-start | bytes 393220
  57.3 2.8 %copy-start.8 = (bf16[1,1,4,128,128]{4,3,2,1,0:T(8,128)(2,1)S(1)}, bf16[1,1,4,128,128]{4,3,2,1,0:T(8,128)(2,1)}, u32[]{:S(2)}) copy-start(bf16[1,1,4,128,128]{4,3,2,1,0:T(8,128)(2,1)} %fusion.29) | copy-start | bytes 393220
  58.0 4.7 %copy-start.3 = (bf16[128,4,128]{2,1,0:T(4,128)(2,1)S(1)}, bf16[128,4,128]{2,1,0:T(4,128)(2,1)}, u32[]{:S(2)}) copy-start(bf16[128,4,128]{2,1,0:T(4,128)(2,1)} %reshape.379) | copy-start | bytes 393220
  58.0 6.6 %collective-permute-start.2 = (bf16[2,1,4,128,128]{4,3,2,1,0:T(8,128)(2,1)}, bf16[2,1,4,128,128]{4,3,2,1,0:T(8,128)(2,1)}, u32[]{:S(2)}, u32[]{:S(2)}) collective-permute-start(bf16[2,1,4,128,128]{4,3,2,1,0:T(8,128)(2,1)} %pad_maximum_fusion.1), channel_id=1, source_target_pairs={{0,1008},{16,0},{32,16},{48,32},{64,48},{80,64},{96,80},{112,96},{... | collective-permute-start | bytes 786440 | tf_op jit(solution)/shard_map/ppermute | solution.py:15
  60.8 14.8 %collective-permute-start.3 = (bf16[2,1,4,128,128]{4,3,2,1,0:T(8,128)(2,1)}, bf16[2,1,4,128,128]{4,3,2,1,0:T(8,128)(2,1)}, u32[]{:S(2)}, u32[]{:S(2)}) collective-permute-start(bf16[2,1,4,128,128]{4,3,2,1,0:T(8,128)(2,1)} %pad_maximum_fusion.2), channel_id=1, source_target_pairs={{0,992},{16,1008},{32,0},{48,16},{64,32},{80,48},{96,64},{112,80},... | collective-permute-start | bytes 786440 | tf_op jit(solution)/shard_map/ppermute | solution.py:15

commit v5 on v4

--- a/solution.py
+++ b/solution.py
@@ -87,11 +87,10 @@
     for step in range(1, CYCLE_STEPS):
         part_query, part_key, part_value = block_grads(blocks[step], masked[step], lse_heads)
         query_sum = query_sum + part_query
-        returned = passed_along(
-            jnp.stack((part_key, part_value)).astype(jnp.bfloat16), "ctx", -step
-        )
-        key_sum = key_sum + returned[0].astype(jnp.float32)
-        value_sum = value_sum + returned[1].astype(jnp.float32)
+        value_back = passed_along(part_value.astype(jnp.bfloat16), "ctx", -step)
+        key_back = passed_along(part_key.astype(jnp.bfloat16), "ctx", -step)
+        key_sum = key_sum + key_back.astype(jnp.float32)
+        value_sum = value_sum + value_back.astype(jnp.float32)
     query_grad = (query_sum * score_scale).astype(jnp.bfloat16).reshape(query.shape)
     flat = (seq_count, tok_rows, KV_HEADS * HEAD_DIM)
     key_grad = jnp.transpose(key_sum.astype(jnp.bfloat16), (0, 3, 1, 2)).reshape(flat)

time: 80.4 us -> 81.8 us (1.017)
  starting transfers between devices: 34.7 us -> 39.4 us
  waiting for transfers between devices: 19.9 us -> 16 us
  other arithmetic: 4.84 us -> 3.38 us
  local copies, waits for them, and re-layouts: 10.2 us -> 11.6 us
    all_to_all x1, waiting for transfers between devices: 8.9 us -> 0.01 us  [shards(): lax.all_to_all(attn_out, 'head', split_axis=0, concat_axis=2, tiled=True)]
    ppermute x4 -> x6, waiting for transfers between devices: 11 us -> 16 us  [passed_along(): return lax.ppermute(value, axis, pairs)]
    ppermute x4 -> x6, starting transfers between devices: 12.5 us -> 17.2 us  [passed_along(): return lax.ppermute(value, axis, pairs)]
    another operation x2 -> x0, other arithmetic: 1.45 us -> none  [shards(): jnp.stack((part_key, part_value)).astype(jnp.bfloat16)]
    another operation x3, local copies, waits for them, and re-layouts: 1.33 us -> 2.33 us
    dot_general x3, matrix products: 3.24 us -> 4.18 us  [block_grads(): jnp.einsum('sgrqk,sqgrd->sgdk', attn_probs.astype(jnp.bfloat16), g5, pref...]
    unnamed x27 -> x23, local copies, waits for them, and re-layouts: 6.1 us -> 6.45 us
  transfers between devices with their start and end apart: 5 -> 7, of which waited for: 2 -> 2; matrix products, arithmetic and copies ran while one was open for 14% -> 19% of each run, Pallas kernels for 0% -> 0%
where the time goes in v5:
time: 81.8 us; the launch traced here: 81.2 us
  starting transfers between devices  39.4 us (48%)
  waiting for transfers between devices  16 us (20%)
  local copies, waits for them, and re-layouts  11.6 us (14%)
  matrix products  9.86 us (12%)
  other arithmetic  3.38 us (4%)
  between operations  0.91 us (1%)
    all_to_all x1, starting transfers between devices, shards(): lax.all_to_all(attn_out, 'head', split_axis=0, concat_axis=2, tiled=True)  22.2 us
    ppermute x6, starting transfers between devices, passed_along(): return lax.ppermute(value, axis, pairs)  17.2 us
    ppermute x6, waiting for transfers between devices, passed_along(): return lax.ppermute(value, axis, pairs)  16 us
    unnamed x23, local copies, waits for them, and re-layouts  6.45 us
    dot_general x3, matrix products, block_grads(): jnp.einsum('sgrqk,sqgrd->sgdk', attn_probs.astype(jnp.bfloat16), g5, pref...  4.18 us
    another operation x3, local copies, waits for them, and re-layouts  2.33 us
    slice x2, local copies, waits for them, and re-layouts, block_grads(): values_here = kv_blk[1].reshape(seq_count, tok_rows, KV_HEADS, HEAD_DIM)  2.32 us
    dot_general x3, matrix products, block_grads(): jnp.einsum('sqgrd,skgd->sgrqk', g5, values_here, preferred_element_type=j...  2.01 us
  transfers between devices with their start and end apart: 7, of which 2 were waited for; matrix products, arithmetic and copies ran while one was open for 19% of the time, Pallas kernels for 0%

profile of v5, /device:TPU:118, one launch (start us, length us, event | category | flops | bytes accessed | tf_op | source)
XLA Modules:
  0.0 81.2 jit_solution(15286549155272549359)
XLA Ops:
  0.6 1.1 %copy.41 = bf16[1,128,512]{1,2,0:T(8,128)(2,1)S(1)} copy(bf16[1,128,512]{2,1,0:T(8,128)(2,1)} %param.8) | data formatting | bytes 262144 | tf_op args[1]
  1.8 0.7 pad_maximum_fusion
  2.6 2.0 %collective-permute-start = (bf16[2,1,128,512]{2,3,1,0:T(8,128)(2,1)}, bf16[2,1,128,512]{2,3,1,0:T(8,128)(2,1)S(1)}, u32[]{:S(2)}, u32[]{:S(2)}) collective-permute-start(bf16[2,1,128,512]{2,3,1,0:T(8,128)(2,1)} %pad_maximum_fusion), channel_id=1, source_target_pairs={{0,16},{16,32},{32,48},{48,64},{64,80},{80,96},{96,112},{112,128},... | collective-permute-start | bytes 786440 | tf_op jit(solution)/shard_map/ppermute | solution.py:15
  4.6 6.6 %collective-permute-start.1 = (bf16[2,1,128,512]{2,3,1,0:T(8,128)(2,1)}, bf16[2,1,128,512]{2,3,1,0:T(8,128)(2,1)}, u32[]{:S(2)}, u32[]{:S(2)}) collective-permute-start(bf16[2,1,128,512]{2,3,1,0:T(8,128)(2,1)} %pad_maximum_fusion), channel_id=1, source_target_pairs={{0,32},{16,48},{32,64},{48,80},{64,96},{80,112},{96,128},{112,144}... | collective-permute-start | bytes 786440 | tf_op jit(solution)/shard_map/ppermute | solution.py:15
  11.3 22.2 %all-to-all-start = ((bf16[16,128,128]{2,1,0:T(8,128)(2,1)}), bf16[16,128,128]{2,1,0:T(8,128)(2,1)}, u32[]{:S(2)}, u32[]{:S(2)}) async-start(bf16[16,128,128]{2,1,0:T(8,128)(2,1)} %param.10), calls=%async_computation | async-start | bytes 1048576 | tf_op jit(solution)/shard_map/all_to_all | solution.py:35
  33.6 0.6 copy-done.8
  34.8 0.4 reshape.278
  35.3 0.5 copy-done.2
  36.3 0.4 fusion.68
  36.7 0.7 fusion.65
  37.4 0.4 fusion.69
  37.7 1.6 %fusion.66 = (bf16[1,1,128,512]{2,3,1,0:T(8,128)(2,1)}, bf16[1,1,128,512]{2,3,1,0:T(8,128)(2,1)S(1)}) fusion(bf16[2,1,128,512]{2,3,1,0:T(8,128)(2,1)} %collective-permute-done.1), kind=kLoop, calls=%fused_computation.96 | loop fusion | bytes 524288 | tf_op jit(solution)/shard_map/slice | solution.py:54
  39.4 0.4 fusion.67
  39.8 0.7 exponential_reduce_fusion.1
  40.5 1.1 %fusion.30 = bf16[1,4,128,128]{3,2,1,0:T(8,128)(2,1)} fusion(f32[1,4,4,128,128]{3,4,2,1,0:T(8,128)S(1)} %get-tuple-element.28, f32[4,4,128]{2,1,0:T(4,128)S(1)} %bitcast.237, bf16[128,4,4,128]{3,2,1,0:T(4,128)(2,1)S(1)} %reshape.282), kind=kOutput, calls=%fused_computation.44 | convolution fusion | flops 67698688 | bytes 1712128 | tf_op jit(solution)/shard_map/sgrqk,sqgrd->sgdk/dot_general | solution.py:67
  41.5 1.1 %fusion.29 = bf16[1,4,128,128]{3,2,1,0:T(8,128)(2,1)} fusion(f32[1,4,4,128,128]{3,4,2,1,0:T(8,128)S(1)} %get-tuple-element.24, f32[4,4,128]{2,1,0:T(4,128)S(1)} %bitcast.238, bf16[128,4,4,128]{3,2,1,0:T(4,128)(2,1)S(1)} %reshape.282), kind=kOutput, calls=%fused_computation.43 | convolution fusion | flops 67698688 | bytes 1712128 | tf_op jit(solution)/shard_map/sgrqk,sqgrd->sgdk/dot_general | solution.py:67
  42.6 2.8 %collective-permute-start.4 = (bf16[1,4,128,128]{3,2,1,0:T(8,128)(2,1)}, bf16[1,4,128,128]{3,2,1,0:T(8,128)(2,1)}, u32[]{:S(2)}, u32[]{:S(2)}) collective-permute-start(bf16[1,4,128,128]{3,2,1,0:T(8,128)(2,1)} %fusion.30), channel_id=1, source_target_pairs={{0,1008},{16,0},{32,16},{48,32},{64,48},{80,64},{96,80},{112,96},{... | collective-permute-start | bytes 393224 | tf_op jit(solution)/shard_map/ppermute | solution.py:15
  45.4 1.9 %collective-permute-start.5 = (bf16[1,4,128,128]{3,2,1,0:T(8,128)(2,1)}, bf16[1,4,128,128]{3,2,1,0:T(8,128)(2,1)}, u32[]{:S(2)}, u32[]{:S(2)}) collective-permute-start(bf16[1,4,128,128]{3,2,1,0:T(8,128)(2,1)} %fusion.29), channel_id=1, source_target_pairs={{0,992},{16,1008},{32,0},{48,16},{64,32},{80,48},{96,64},{112,80},... | collective-permute-start | bytes 393224 | tf_op jit(solution)/shard_map/ppermute | solution.py:15
  47.3 1.6 %reshape.281 = bf16[128,4,128]{2,1,0:T(4,128)(2,1)} reshape(bf16[1,128,512]{2,1,0:T(8,128)(2,1)} %param.9) | data formatting | bytes 262144 | tf_op jit(solution)/shard_map/reshape.21
  48.9 7.6 %collective-permute-done.5 = bf16[1,4,128,128]{3,2,1,0:T(8,128)(2,1)} collective-permute-done((bf16[1,4,128,128]{3,2,1,0:T(8,128)(2,1)}, bf16[1,4,128,128]{3,2,1,0:T(8,128)(2,1)}, u32[]{:S(2)}, u32[]{:S(2)}) %collective-permute-start.5) | collective-permute-done | bytes 131104 | tf_op jit(solution)/shard_map/ppermute | solution.py:15
  56.5 2.0 %add_convert_fusion = bf16[1,4,128,128]{3,2,1,0:T(8,128)(2,1)} fusion(bf16[1,4,128,128]{3,2,1,0:T(8,128)(2,1)} %collective-permute-done.5, bf16[1,4,128,128]{3,2,1,0:T(8,128)(2,1)} %collective-permute-done.4, bf16[128,4,4,128]{3,2,1,0:T(4,128)(2,1)S(1)} %reshape.282, f32[1,4,4,128,128]{3,4,2,1,0:T(8,128)S(1)} %get-tuple-element.26, ...), kind=kOutput, calls=%fused_computation.67 | convolution fusion | flops 67960832 | bytes 1974272 | tf_op jit(solution)/shard_map/sgrqk,sqgrd->sgdk/dot_general | solution.py:67
  58.6 1.7 %copy.72 = bf16[1,128,512]{2,1,0:T(8,128)(2,1)} copy(bf16[1,128,512]{1,2,0:T(8,128)(2,1)} %bitcast.236) | data formatting | bytes 262144
  60.2 1.6 %fusion.33 = f32[128,16]{0,1:T(8,128)S(1)} fusion(bf16[16,128,128]{2,1,0:T(8,128)(2,1)} %all-to-all-done, bf16[1,128,2048]{2,1,0:T(8,128)(2,1)} %param.11), kind=kLoop, calls=%fused_computation.48 | loop fusion | flops 1046528 | bytes 1056768 | tf_op jit(solution)/shard_map/reduce_sum | solution.py:40
  61.9 1.3 %fusion.20 = bf16[4,4,128,128]{2,3,1,0:T(8,128)(2,1)S(1)} fusion(bf16[128,4,128,1]{0,2,3,1:T(8,128)(2,1)} %bitcast.232, f32[1,4,4,128,128]{3,4,2,1,0:T(8,128)S(1)} %copy-done.1, f32[4,4,128]{2,1,0:T(4,128)S(1)} %bitcast.243, f32[4,4,128]{2,1,0:T(4,128)S(1)} %bitcast.240, bf16[128,4,4,128]{3,2,1,0:T(4,128)(2,1)S(1)} %reshape.282), kind=kOutput, calls=%fused_computation.28 | convolution fusion | flops 68157440 | bytes 2244608 | tf_op jit(solution)/shard_map/sqgrd,skgd->sgrqk/dot_general | solution.py:56
  63.2 1.0 %fusion.32 = bf16[1,4,128,128]{3,2,1,0:T(8,128)(2,1)} fusion(bf16[4,4,128,128]{2,3,1,0:T(8,128)(2,1)S(1)} %fusion.20, bf16[128,4,4,128]{3,2,1,0:T(4,128)(2,1)S(1)} %reshape.278), kind=kOutput, calls=%fused_computation.46 | convolution fusion | flops 67239936 | bytes 1179648 | tf_op jit(solution)/shard_map/sgrqk,sqgrd->sgdk/dot_general | solution.py:64
  64.5 0.6 copy-done.7
  65.1 0.4 fusion.19
  65.9 1.9 %collective-permute-start.2 = (bf16[1,4,128,128]{3,2,1,0:T(8,128)(2,1)S(1)}, bf16[1,4,128,128]{3,2,1,0:T(8,128)(2,1)S(1)}, u32[]{:S(2)}, u32[]{:S(2)}) collective-permute-start(bf16[1,4,128,128]{3,2,1,0:T(8,128)(2,1)S(1)} %fusion.31), channel_id=1, source_target_pairs={{0,1008},{16,0},{32,16},{48,32},{64,48},{80,64},{96,80},{112,96},{... | collective-permute-start | bytes 393224 | tf_op jit(solution)/shard_map/ppermute | solution.py:15
  68.1 1.9 %collective-permute-start.3 = (bf16[1,4,128,128]{3,2,1,0:T(8,128)(2,1)}, bf16[1,4,128,128]{3,2,1,0:T(8,128)(2,1)S(1)}, u32[]{:S(2)}, u32[]{:S(2)}) collective-permute-start(bf16[1,4,128,128]{3,2,1,0:T(8,128)(2,1)} %fusion.32), channel_id=1, source_target_pairs={{0,992},{16,1008},{32,0},{48,16},{64,32},{80,48},{96,64},{112,80},... | collective-permute-start | bytes 393224 | tf_op jit(solution)/shard_map/ppermute | solution.py:15
  70.7 1.0 %copy.70 = bf16[1,128,2048]{2,1,0:T(8,128)(2,1)} copy(bf16[1,128,2048]{1,2,0:T(8,128)(2,1)S(1)} %bitcast.225) | data formatting | bytes 1048576
  71.7 8.4 %collective-permute-done.3 = bf16[1,4,128,128]{3,2,1,0:T(8,128)(2,1)S(1)} collective-permute-done((bf16[1,4,128,128]{3,2,1,0:T(8,128)(2,1)}, bf16[1,4,128,128]{3,2,1,0:T(8,128)(2,1)S(1)}, u32[]{:S(2)}, u32[]{:S(2)}) %collective-permute-start.3) | collective-permute-done | bytes 131104 | tf_op jit(solution)/shard_map/ppermute | solution.py:15
  80.4 0.8 copy.71
  (40 shorter events, 3.3 us)
Async XLA Ops:
  0.6 1.1 %copy-start.6 = (bf16[1,128,512]{2,1,0:T(8,128)(2,1)S(1)}, bf16[1,128,512]{2,1,0:T(8,128)(2,1)}, u32[]{:S(2)}) copy-start(bf16[1,128,512]{2,1,0:T(8,128)(2,1)} %param.9) | copy-start | bytes 393220
  2.6 32.2 %copy-start.4 = (bf16[1,128,2048]{2,1,0:T(8,128)(2,1)S(1)}, bf16[1,128,2048]{2,1,0:T(8,128)(2,1)}, u32[]{:S(2)}) copy-start(bf16[1,128,2048]{2,1,0:T(8,128)(2,1)} %param.7) | copy-start | bytes 1572868
  2.6 34.1 %collective-permute-start = (bf16[2,1,128,512]{2,3,1,0:T(8,128)(2,1)}, bf16[2,1,128,512]{2,3,1,0:T(8,128)(2,1)S(1)}, u32[]{:S(2)}, u32[]{:S(2)}) collective-permute-start(bf16[2,1,128,512]{2,3,1,0:T(8,128)(2,1)} %pad_maximum_fusion), channel_id=1, source_target_pairs={{0,16},{16,32},{32,48},{48,64},{64,80},{80,96},{96,112},{112,128},... | collective-permute-start | bytes 786440 | tf_op jit(solution)/shard_map/ppermute | solution.py:15
  4.6 33.1 %collective-permute-start.1 = (bf16[2,1,128,512]{2,3,1,0:T(8,128)(2,1)}, bf16[2,1,128,512]{2,3,1,0:T(8,128)(2,1)}, u32[]{:S(2)}, u32[]{:S(2)}) collective-permute-start(bf16[2,1,128,512]{2,3,1,0:T(8,128)(2,1)} %pad_maximum_fusion), channel_id=1, source_target_pairs={{0,32},{16,48},{32,64},{48,80},{64,96},{80,112},{96,128},{112,144}... | collective-permute-start | bytes 786440 | tf_op jit(solution)/shard_map/ppermute | solution.py:15
  11.3 22.2 %copy-start.5 = (bf16[1,128,512]{2,1,0:T(8,128)(2,1)S(1)}, bf16[1,128,512]{2,1,0:T(8,128)(2,1)}, u32[]{:S(2)}) copy-start(bf16[1,128,512]{2,1,0:T(8,128)(2,1)} %param.8) | copy-start | bytes 393220
  11.3 49.0 %all-to-all-start = ((bf16[16,128,128]{2,1,0:T(8,128)(2,1)}), bf16[16,128,128]{2,1,0:T(8,128)(2,1)}, u32[]{:S(2)}, u32[]{:S(2)}) async-start(bf16[16,128,128]{2,1,0:T(8,128)(2,1)} %param.10), calls=%async_computation | async-start | bytes 1048576 | tf_op jit(solution)/shard_map/all_to_all | solution.py:35
  33.5 0.7 copy-start.8
  34.8 1.0 %copy-start.2 = (bf16[1,128,2048]{2,1,0:T(8,128)(2,1)S(1)}, bf16[1,128,2048]{2,1,0:T(8,128)(2,1)}, u32[]{:S(2)}) copy-start(bf16[1,128,2048]{2,1,0:T(8,128)(2,1)} %param.11) | copy-start | bytes 1572868
  39.8 1.8 %copy-start = (f32[1,4,4,128,128]{3,4,2,1,0:T(8,128)}, f32[1,4,4,128,128]{3,4,2,1,0:T(8,128)S(1)}, u32[]{:S(2)}) copy-start(f32[1,4,4,128,128]{3,4,2,1,0:T(8,128)S(1)} %get-tuple-element.24) | copy-start | bytes 3145732
  42.6 6.3 %collective-permute-start.4 = (bf16[1,4,128,128]{3,2,1,0:T(8,128)(2,1)}, bf16[1,4,128,128]{3,2,1,0:T(8,128)(2,1)}, u32[]{:S(2)}, u32[]{:S(2)}) collective-permute-start(bf16[1,4,128,128]{3,2,1,0:T(8,128)(2,1)} %fusion.30), channel_id=1, source_target_pairs={{0,1008},{16,0},{32,16},{48,32},{64,48},{80,64},{96,80},{112,96},{... | collective-permute-start | bytes 393224 | tf_op jit(solution)/shard_map/ppermute | solution.py:15
  45.4 11.1 %collective-permute-start.5 = (bf16[1,4,128,128]{3,2,1,0:T(8,128)(2,1)}, bf16[1,4,128,128]{3,2,1,0:T(8,128)(2,1)}, u32[]{:S(2)}, u32[]{:S(2)}) collective-permute-start(bf16[1,4,128,128]{3,2,1,0:T(8,128)(2,1)} %fusion.29), channel_id=1, source_target_pairs={{0,992},{16,1008},{32,0},{48,16},{64,32},{80,48},{96,64},{112,80},... | collective-permute-start | bytes 393224 | tf_op jit(solution)/shard_map/ppermute | solution.py:15
  60.2 1.6 %copy-start.1 = (f32[1,4,4,128,128]{3,4,2,1,0:T(8,128)S(1)}, f32[1,4,4,128,128]{3,4,2,1,0:T(8,128)}, u32[]{:S(2)}) copy-start(f32[1,4,4,128,128]{3,4,2,1,0:T(8,128)} %copy-done) | copy-start | bytes 3145732
  64.2 0.9 %copy-start.7 = (bf16[1,1,128,512]{2,3,1,0:T(8,128)(2,1)S(1)}, bf16[1,1,128,512]{2,3,1,0:T(8,128)(2,1)}, u32[]{:S(2)}) copy-start(bf16[1,1,128,512]{2,3,1,0:T(8,128)(2,1)} %get-tuple-element.12) | copy-start | bytes 393220
  65.5 2.3 %copy-start.3 = (bf16[128,4,128]{2,1,0:T(4,128)(2,1)S(1)}, bf16[128,4,128]{2,1,0:T(4,128)(2,1)}, u32[]{:S(2)}) copy-start(bf16[128,4,128]{2,1,0:T(4,128)(2,1)} %reshape.281) | copy-start | bytes 393220
  65.9 5.8 %collective-permute-start.2 = (bf16[1,4,128,128]{3,2,1,0:T(8,128)(2,1)S(1)}, bf16[1,4,128,128]{3,2,1,0:T(8,128)(2,1)S(1)}, u32[]{:S(2)}, u32[]{:S(2)}) collective-permute-start(bf16[1,4,128,128]{3,2,1,0:T(8,128)(2,1)S(1)} %fusion.31), channel_id=1, source_target_pairs={{0,1008},{16,0},{32,16},{48,32},{64,48},{80,64},{96,80},{112,96},{... | collective-permute-start | bytes 393224 | tf_op jit(solution)/shard_map/ppermute | solution.py:15
  68.1 11.9 %collective-permute-start.3 = (bf16[1,4,128,128]{3,2,1,0:T(8,128)(2,1)}, bf16[1,4,128,128]{3,2,1,0:T(8,128)(2,1)S(1)}, u32[]{:S(2)}, u32[]{:S(2)}) collective-permute-start(bf16[1,4,128,128]{3,2,1,0:T(8,128)(2,1)} %fusion.32), channel_id=1, source_target_pairs={{0,992},{16,1008},{32,0},{48,16},{64,32},{80,48},{96,64},{112,80},... | collective-permute-start | bytes 393224 | tf_op jit(solution)/shard_map/ppermute | solution.py:15

commit v6 on v5

--- a/solution.py
+++ b/solution.py
@@ -15,7 +15,7 @@
     return lax.ppermute(value, axis, pairs)
 
 
-def shards(query, key, value, attn_out, grad_out, logsumexp, span_order):
+def shards_body(query, key, value, attn_out, grad_out, logsumexp, span_order):
     cycle_size = lax.axis_size("ctx")
     here = lax.axis_index("ctx")
     seq_count = query.shape[0]
@@ -30,7 +30,9 @@
         return (starts[:, None] + offsets[None, :]).reshape(tok_rows)
 
     own_kv = jnp.stack((key, value))
-    kv_ahead = [passed_along(own_kv, "ctx", step) for step in range(1, CYCLE_STEPS)]
+    kv_ahead = []
+    for step in range(1, CYCLE_STEPS):
+        kv_ahead.append(passed_along(own_kv, "ctx", step))
 
     outputs = lax.all_to_all(attn_out, "head", split_axis=0, concat_axis=2, tiled=True)
 
@@ -109,4 +111,4 @@
         P(),
     )
     out_specs = (P("head", "ctx", None), P("head", "ctx", None), P("head", "ctx", None))
-    return jax.shard_map(shards, mesh=mesh, in_specs=in_specs, out_specs=out_specs, check_vma=False)
+    return jax.shard_map(shards_body, mesh=mesh, in_specs=in_specs, out_specs=out_specs, check_vma=False)

time: 81.8 us -> 81.8 us (level)
  no operation moved by 1% of the time
where the time goes in v6:
time: 81.8 us; the launch traced here: 81.2 us
  starting transfers between devices  39.4 us (48%)
  waiting for transfers between devices  16 us (20%)
  local copies, waits for them, and re-layouts  11.6 us (14%)
  matrix products  9.86 us (12%)
  other arithmetic  3.38 us (4%)
  between operations  0.91 us (1%)
    all_to_all x1, starting transfers between devices, shards_body(): lax.all_to_all(attn_out, 'head', split_axis=0, concat_axis=2, tiled=True)  22.2 us
    ppermute x6, starting transfers between devices, passed_along(): return lax.ppermute(value, axis, pairs)  17.2 us
    ppermute x6, waiting for transfers between devices, passed_along(): return lax.ppermute(value, axis, pairs)  16 us
    unnamed x23, local copies, waits for them, and re-layouts  6.45 us
    dot_general x3, matrix products, block_grads(): jnp.einsum('sgrqk,sqgrd->sgdk', attn_probs.astype(jnp.bfloat16), g5, pref...  4.18 us
    another operation x3, local copies, waits for them, and re-layouts  2.33 us
    slice x2, local copies, waits for them, and re-layouts, block_grads(): values_here = kv_blk[1].reshape(seq_count, tok_rows, KV_HEADS, HEAD_DIM)  2.32 us
    dot_general x3, matrix products, block_grads(): jnp.einsum('sqgrd,skgd->sgrqk', g5, values_here, preferred_element_type=j...  2.01 us
  transfers between devices with their start and end apart: 7, of which 2 were waited for; matrix products, arithmetic and copies ran while one was open for 19% of the time, Pallas kernels for 0%

profile of v6, /device:TPU:118, one launch (start us, length us, event | category | flops | bytes accessed | tf_op | source)
XLA Modules:
  0.0 81.2 jit_solution(15286549155272549359)
XLA Ops:
  0.6 1.1 %copy.41 = bf16[1,128,512]{1,2,0:T(8,128)(2,1)S(1)} copy(bf16[1,128,512]{2,1,0:T(8,128)(2,1)} %param.8) | data formatting | bytes 262144 | tf_op args[1]
  1.8 0.7 pad_maximum_fusion
  2.6 2.0 %collective-permute-start = (bf16[2,1,128,512]{2,3,1,0:T(8,128)(2,1)}, bf16[2,1,128,512]{2,3,1,0:T(8,128)(2,1)S(1)}, u32[]{:S(2)}, u32[]{:S(2)}) collective-permute-start(bf16[2,1,128,512]{2,3,1,0:T(8,128)(2,1)} %pad_maximum_fusion), channel_id=1, source_target_pairs={{0,16},{16,32},{32,48},{48,64},{64,80},{80,96},{96,112},{112,128},... | collective-permute-start | bytes 786440 | tf_op jit(solution)/shard_map/ppermute | solution.py:15
  4.6 6.6 %collective-permute-start.1 = (bf16[2,1,128,512]{2,3,1,0:T(8,128)(2,1)}, bf16[2,1,128,512]{2,3,1,0:T(8,128)(2,1)}, u32[]{:S(2)}, u32[]{:S(2)}) collective-permute-start(bf16[2,1,128,512]{2,3,1,0:T(8,128)(2,1)} %pad_maximum_fusion), channel_id=1, source_target_pairs={{0,32},{16,48},{32,64},{48,80},{64,96},{80,112},{96,128},{112,144}... | collective-permute-start | bytes 786440 | tf_op jit(solution)/shard_map/ppermute | solution.py:15
  11.3 22.2 %all-to-all-start = ((bf16[16,128,128]{2,1,0:T(8,128)(2,1)}), bf16[16,128,128]{2,1,0:T(8,128)(2,1)}, u32[]{:S(2)}, u32[]{:S(2)}) async-start(bf16[16,128,128]{2,1,0:T(8,128)(2,1)} %param.10), calls=%async_computation | async-start | bytes 1048576 | tf_op jit(solution)/shard_map/all_to_all | solution.py:37
  33.6 0.6 copy-done.8
  34.8 0.4 reshape.278
  35.3 0.5 copy-done.2
  36.3 0.4 fusion.68
  36.7 0.7 fusion.65
  37.4 0.4 fusion.69
  37.7 1.6 %fusion.66 = (bf16[1,1,128,512]{2,3,1,0:T(8,128)(2,1)}, bf16[1,1,128,512]{2,3,1,0:T(8,128)(2,1)S(1)}) fusion(bf16[2,1,128,512]{2,3,1,0:T(8,128)(2,1)} %collective-permute-done.1), kind=kLoop, calls=%fused_computation.96 | loop fusion | bytes 524288 | tf_op jit(solution)/shard_map/slice | solution.py:56
  39.4 0.4 fusion.67
  39.8 0.7 exponential_reduce_fusion.1
  40.5 1.1 %fusion.30 = bf16[1,4,128,128]{3,2,1,0:T(8,128)(2,1)} fusion(f32[1,4,4,128,128]{3,4,2,1,0:T(8,128)S(1)} %get-tuple-element.28, f32[4,4,128]{2,1,0:T(4,128)S(1)} %bitcast.237, bf16[128,4,4,128]{3,2,1,0:T(4,128)(2,1)S(1)} %reshape.282), kind=kOutput, calls=%fused_computation.44 | convolution fusion | flops 67698688 | bytes 1712128 | tf_op jit(solution)/shard_map/sgrqk,sqgrd->sgdk/dot_general | solution.py:69
  41.5 1.1 %fusion.29 = bf16[1,4,128,128]{3,2,1,0:T(8,128)(2,1)} fusion(f32[1,4,4,128,128]{3,4,2,1,0:T(8,128)S(1)} %get-tuple-element.24, f32[4,4,128]{2,1,0:T(4,128)S(1)} %bitcast.238, bf16[128,4,4,128]{3,2,1,0:T(4,128)(2,1)S(1)} %reshape.282), kind=kOutput, calls=%fused_computation.43 | convolution fusion | flops 67698688 | bytes 1712128 | tf_op jit(solution)/shard_map/sgrqk,sqgrd->sgdk/dot_general | solution.py:69
  42.6 2.8 %collective-permute-start.4 = (bf16[1,4,128,128]{3,2,1,0:T(8,128)(2,1)}, bf16[1,4,128,128]{3,2,1,0:T(8,128)(2,1)}, u32[]{:S(2)}, u32[]{:S(2)}) collective-permute-start(bf16[1,4,128,128]{3,2,1,0:T(8,128)(2,1)} %fusion.30), channel_id=1, source_target_pairs={{0,1008},{16,0},{32,16},{48,32},{64,48},{80,64},{96,80},{112,96},{... | collective-permute-start | bytes 393224 | tf_op jit(solution)/shard_map/ppermute | solution.py:15
  45.4 1.9 %collective-permute-start.5 = (bf16[1,4,128,128]{3,2,1,0:T(8,128)(2,1)}, bf16[1,4,128,128]{3,2,1,0:T(8,128)(2,1)}, u32[]{:S(2)}, u32[]{:S(2)}) collective-permute-start(bf16[1,4,128,128]{3,2,1,0:T(8,128)(2,1)} %fusion.29), channel_id=1, source_target_pairs={{0,992},{16,1008},{32,0},{48,16},{64,32},{80,48},{96,64},{112,80},... | collective-permute-start | bytes 393224 | tf_op jit(solution)/shard_map/ppermute | solution.py:15
  47.3 1.6 %reshape.281 = bf16[128,4,128]{2,1,0:T(4,128)(2,1)} reshape(bf16[1,128,512]{2,1,0:T(8,128)(2,1)} %param.9) | data formatting | bytes 262144 | tf_op jit(solution)/shard_map/reshape.21
  48.9 7.6 %collective-permute-done.5 = bf16[1,4,128,128]{3,2,1,0:T(8,128)(2,1)} collective-permute-done((bf16[1,4,128,128]{3,2,1,0:T(8,128)(2,1)}, bf16[1,4,128,128]{3,2,1,0:T(8,128)(2,1)}, u32[]{:S(2)}, u32[]{:S(2)}) %collective-permute-start.5) | collective-permute-done | bytes 131104 | tf_op jit(solution)/shard_map/ppermute | solution.py:15
  56.5 2.0 %add_convert_fusion = bf16[1,4,128,128]{3,2,1,0:T(8,128)(2,1)} fusion(bf16[1,4,128,128]{3,2,1,0:T(8,128)(2,1)} %collective-permute-done.5, bf16[1,4,128,128]{3,2,1,0:T(8,128)(2,1)} %collective-permute-done.4, bf16[128,4,4,128]{3,2,1,0:T(4,128)(2,1)S(1)} %reshape.282, f32[1,4,4,128,128]{3,4,2,1,0:T(8,128)S(1)} %get-tuple-element.26, ...), kind=kOutput, calls=%fused_computation.67 | convolution fusion | flops 67960832 | bytes 1974272 | tf_op jit(solution)/shard_map/sgrqk,sqgrd->sgdk/dot_general | solution.py:69
  58.6 1.7 %copy.72 = bf16[1,128,512]{2,1,0:T(8,128)(2,1)} copy(bf16[1,128,512]{1,2,0:T(8,128)(2,1)} %bitcast.236) | data formatting | bytes 262144
  60.2 1.6 %fusion.33 = f32[128,16]{0,1:T(8,128)S(1)} fusion(bf16[16,128,128]{2,1,0:T(8,128)(2,1)} %all-to-all-done, bf16[1,128,2048]{2,1,0:T(8,128)(2,1)} %param.11), kind=kLoop, calls=%fused_computation.48 | loop fusion | flops 1046528 | bytes 1056768 | tf_op jit(solution)/shard_map/reduce_sum | solution.py:42
  61.9 1.3 %fusion.20 = bf16[4,4,128,128]{2,3,1,0:T(8,128)(2,1)S(1)} fusion(bf16[128,4,128,1]{0,2,3,1:T(8,128)(2,1)} %bitcast.232, f32[1,4,4,128,128]{3,4,2,1,0:T(8,128)S(1)} %copy-done.1, f32[4,4,128]{2,1,0:T(4,128)S(1)} %bitcast.243, f32[4,4,128]{2,1,0:T(4,128)S(1)} %bitcast.240, bf16[128,4,4,128]{3,2,1,0:T(4,128)(2,1)S(1)} %reshape.282), kind=kOutput, calls=%fused_computation.28 | convolution fusion | flops 68157440 | bytes 2244608 | tf_op jit(solution)/shard_map/sqgrd,skgd->sgrqk/dot_general | solution.py:58
  63.2 1.0 %fusion.32 = bf16[1,4,128,128]{3,2,1,0:T(8,128)(2,1)} fusion(bf16[4,4,128,128]{2,3,1,0:T(8,128)(2,1)S(1)} %fusion.20, bf16[128,4,4,128]{3,2,1,0:T(4,128)(2,1)S(1)} %reshape.278), kind=kOutput, calls=%fused_computation.46 | convolution fusion | flops 67239936 | bytes 1179648 | tf_op jit(solution)/shard_map/sgrqk,sqgrd->sgdk/dot_general | solution.py:66
  64.5 0.6 copy-done.7
  65.1 0.4 fusion.19
  65.9 1.9 %collective-permute-start.2 = (bf16[1,4,128,128]{3,2,1,0:T(8,128)(2,1)S(1)}, bf16[1,4,128,128]{3,2,1,0:T(8,128)(2,1)S(1)}, u32[]{:S(2)}, u32[]{:S(2)}) collective-permute-start(bf16[1,4,128,128]{3,2,1,0:T(8,128)(2,1)S(1)} %fusion.31), channel_id=1, source_target_pairs={{0,1008},{16,0},{32,16},{48,32},{64,48},{80,64},{96,80},{112,96},{... | collective-permute-start | bytes 393224 | tf_op jit(solution)/shard_map/ppermute | solution.py:15
  68.1 1.9 %collective-permute-start.3 = (bf16[1,4,128,128]{3,2,1,0:T(8,128)(2,1)}, bf16[1,4,128,128]{3,2,1,0:T(8,128)(2,1)S(1)}, u32[]{:S(2)}, u32[]{:S(2)}) collective-permute-start(bf16[1,4,128,128]{3,2,1,0:T(8,128)(2,1)} %fusion.32), channel_id=1, source_target_pairs={{0,992},{16,1008},{32,0},{48,16},{64,32},{80,48},{96,64},{112,80},... | collective-permute-start | bytes 393224 | tf_op jit(solution)/shard_map/ppermute | solution.py:15
  70.7 1.0 %copy.70 = bf16[1,128,2048]{2,1,0:T(8,128)(2,1)} copy(bf16[1,128,2048]{1,2,0:T(8,128)(2,1)S(1)} %bitcast.225) | data formatting | bytes 1048576
  71.7 8.4 %collective-permute-done.3 = bf16[1,4,128,128]{3,2,1,0:T(8,128)(2,1)S(1)} collective-permute-done((bf16[1,4,128,128]{3,2,1,0:T(8,128)(2,1)}, bf16[1,4,128,128]{3,2,1,0:T(8,128)(2,1)S(1)}, u32[]{:S(2)}, u32[]{:S(2)}) %collective-permute-start.3) | collective-permute-done | bytes 131104 | tf_op jit(solution)/shard_map/ppermute | solution.py:15
  80.4 0.8 copy.71
  (40 shorter events, 3.3 us)
Async XLA Ops:
  0.6 1.1 %copy-start.6 = (bf16[1,128,512]{2,1,0:T(8,128)(2,1)S(1)}, bf16[1,128,512]{2,1,0:T(8,128)(2,1)}, u32[]{:S(2)}) copy-start(bf16[1,128,512]{2,1,0:T(8,128)(2,1)} %param.9) | copy-start | bytes 393220
  2.6 32.2 %copy-start.4 = (bf16[1,128,2048]{2,1,0:T(8,128)(2,1)S(1)}, bf16[1,128,2048]{2,1,0:T(8,128)(2,1)}, u32[]{:S(2)}) copy-start(bf16[1,128,2048]{2,1,0:T(8,128)(2,1)} %param.7) | copy-start | bytes 1572868
  2.6 34.1 %collective-permute-start = (bf16[2,1,128,512]{2,3,1,0:T(8,128)(2,1)}, bf16[2,1,128,512]{2,3,1,0:T(8,128)(2,1)S(1)}, u32[]{:S(2)}, u32[]{:S(2)}) collective-permute-start(bf16[2,1,128,512]{2,3,1,0:T(8,128)(2,1)} %pad_maximum_fusion), channel_id=1, source_target_pairs={{0,16},{16,32},{32,48},{48,64},{64,80},{80,96},{96,112},{112,128},... | collective-permute-start | bytes 786440 | tf_op jit(solution)/shard_map/ppermute | solution.py:15
  4.6 33.1 %collective-permute-start.1 = (bf16[2,1,128,512]{2,3,1,0:T(8,128)(2,1)}, bf16[2,1,128,512]{2,3,1,0:T(8,128)(2,1)}, u32[]{:S(2)}, u32[]{:S(2)}) collective-permute-start(bf16[2,1,128,512]{2,3,1,0:T(8,128)(2,1)} %pad_maximum_fusion), channel_id=1, source_target_pairs={{0,32},{16,48},{32,64},{48,80},{64,96},{80,112},{96,128},{112,144}... | collective-permute-start | bytes 786440 | tf_op jit(solution)/shard_map/ppermute | solution.py:15
  11.3 22.2 %copy-start.5 = (bf16[1,128,512]{2,1,0:T(8,128)(2,1)S(1)}, bf16[1,128,512]{2,1,0:T(8,128)(2,1)}, u32[]{:S(2)}) copy-start(bf16[1,128,512]{2,1,0:T(8,128)(2,1)} %param.8) | copy-start | bytes 393220
  11.3 49.0 %all-to-all-start = ((bf16[16,128,128]{2,1,0:T(8,128)(2,1)}), bf16[16,128,128]{2,1,0:T(8,128)(2,1)}, u32[]{:S(2)}, u32[]{:S(2)}) async-start(bf16[16,128,128]{2,1,0:T(8,128)(2,1)} %param.10), calls=%async_computation | async-start | bytes 1048576 | tf_op jit(solution)/shard_map/all_to_all | solution.py:37
  33.5 0.7 copy-start.8
  34.8 1.0 %copy-start.2 = (bf16[1,128,2048]{2,1,0:T(8,128)(2,1)S(1)}, bf16[1,128,2048]{2,1,0:T(8,128)(2,1)}, u32[]{:S(2)}) copy-start(bf16[1,128,2048]{2,1,0:T(8,128)(2,1)} %param.11) | copy-start | bytes 1572868
  39.8 1.8 %copy-start = (f32[1,4,4,128,128]{3,4,2,1,0:T(8,128)}, f32[1,4,4,128,128]{3,4,2,1,0:T(8,128)S(1)}, u32[]{:S(2)}) copy-start(f32[1,4,4,128,128]{3,4,2,1,0:T(8,128)S(1)} %get-tuple-element.24) | copy-start | bytes 3145732
  42.6 6.3 %collective-permute-start.4 = (bf16[1,4,128,128]{3,2,1,0:T(8,128)(2,1)}, bf16[1,4,128,128]{3,2,1,0:T(8,128)(2,1)}, u32[]{:S(2)}, u32[]{:S(2)}) collective-permute-start(bf16[1,4,128,128]{3,2,1,0:T(8,128)(2,1)} %fusion.30), channel_id=1, source_target_pairs={{0,1008},{16,0},{32,16},{48,32},{64,48},{80,64},{96,80},{112,96},{... | collective-permute-start | bytes 393224 | tf_op jit(solution)/shard_map/ppermute | solution.py:15
  45.4 11.1 %collective-permute-start.5 = (bf16[1,4,128,128]{3,2,1,0:T(8,128)(2,1)}, bf16[1,4,128,128]{3,2,1,0:T(8,128)(2,1)}, u32[]{:S(2)}, u32[]{:S(2)}) collective-permute-start(bf16[1,4,128,128]{3,2,1,0:T(8,128)(2,1)} %fusion.29), channel_id=1, source_target_pairs={{0,992},{16,1008},{32,0},{48,16},{64,32},{80,48},{96,64},{112,80},... | collective-permute-start | bytes 393224 | tf_op jit(solution)/shard_map/ppermute | solution.py:15
  60.2 1.6 %copy-start.1 = (f32[1,4,4,128,128]{3,4,2,1,0:T(8,128)S(1)}, f32[1,4,4,128,128]{3,4,2,1,0:T(8,128)}, u32[]{:S(2)}) copy-start(f32[1,4,4,128,128]{3,4,2,1,0:T(8,128)} %copy-done) | copy-start | bytes 3145732
  64.2 0.9 %copy-start.7 = (bf16[1,1,128,512]{2,3,1,0:T(8,128)(2,1)S(1)}, bf16[1,1,128,512]{2,3,1,0:T(8,128)(2,1)}, u32[]{:S(2)}) copy-start(bf16[1,1,128,512]{2,3,1,0:T(8,128)(2,1)} %get-tuple-element.12) | copy-start | bytes 393220
  65.5 2.3 %copy-start.3 = (bf16[128,4,128]{2,1,0:T(4,128)(2,1)S(1)}, bf16[128,4,128]{2,1,0:T(4,128)(2,1)}, u32[]{:S(2)}) copy-start(bf16[128,4,128]{2,1,0:T(4,128)(2,1)} %reshape.281) | copy-start | bytes 393220
  65.9 5.8 %collective-permute-start.2 = (bf16[1,4,128,128]{3,2,1,0:T(8,128)(2,1)S(1)}, bf16[1,4,128,128]{3,2,1,0:T(8,128)(2,1)S(1)}, u32[]{:S(2)}, u32[]{:S(2)}) collective-permute-start(bf16[1,4,128,128]{3,2,1,0:T(8,128)(2,1)S(1)} %fusion.31), channel_id=1, source_target_pairs={{0,1008},{16,0},{32,16},{48,32},{64,48},{80,64},{96,80},{112,96},{... | collective-permute-start | bytes 393224 | tf_op jit(solution)/shard_map/ppermute | solution.py:15
  68.1 11.9 %collective-permute-start.3 = (bf16[1,4,128,128]{3,2,1,0:T(8,128)(2,1)}, bf16[1,4,128,128]{3,2,1,0:T(8,128)(2,1)S(1)}, u32[]{:S(2)}, u32[]{:S(2)}) collective-permute-start(bf16[1,4,128,128]{3,2,1,0:T(8,128)(2,1)} %fusion.32), channel_id=1, source_target_pairs={{0,992},{16,1008},{32,0},{48,16},{64,32},{80,48},{96,64},{112,80},... | collective-permute-start | bytes 393224 | tf_op jit(solution)/shard_map/ppermute | solution.py:15
